TPU v7x, 32 devices: a whole 2x2x4 slice. The times are simulated.
32 devices in a mesh: section: 4 (over x, core), ctx: 8 (over z, y).
Axes of the slice: x: 2, y: 2, z: 4, core: 2. Of those that a mesh axis runs over, the one named last changes fastest.
Arguments:
- block_order: int32 [8], replicated, may hold values from 0 to 7, each once
- queries: bfloat16 [4, 64, 2560], P('section', 'ctx'), may hold values from -400 to 400
- cache_keys: bfloat16 [1024, 2560], P('ctx', 'section'), may hold values from -6 to 6
- cache_values: bfloat16 [1024, 2560], P('ctx', 'section'), may hold values from -6 to 6
- attention_out: bfloat16 [4, 64, 2560], P('section', 'ctx'), may hold values from -6 to 6
- output_grad: bfloat16 [4, 64, 2560], P('section', 'ctx'), may hold values from -192 to 192
Outputs:
- grad_queries: bfloat16 [4, 64, 2560], P('section', 'ctx')
- grad_keys: bfloat16 [1024, 2560], P('ctx', 'section')
- grad_values: bfloat16 [1024, 2560], P('ctx', 'section')
Inputs may be any that keep to these rules, and one draw needn't show every extreme that they name: `block_order`: every block number once.
All inputs are finite; a program needn't handle non-finite values.
Results may differ from a plain program's by a relative error of at most 0.012.
Values may be sent and summed in bfloat16 or wider, within the bound.
No kernel may reach another device: no remote copies, remote signals or barrier semaphores. Data moves between devices by JAX's collectives and lax.ppermute only.
A program may use at most 64 MiB of HBM per device.

v0:
```python
import math

import jax
import jax.numpy as jnp
from jax import lax
from jax.experimental import pallas as pl
from jax.experimental.pallas import tpu as pltpu
from jax.sharding import PartitionSpec as P


HEAD_DIM = 128
LANES = 128
ON_CHIP_BYTES = 1 << 20
masked_score = -1e30
BF = jnp.bfloat16
F32 = jnp.float32


def nt(a, b):
    return lax.dot_general(a, b, (((1,), (1,)), ((), ())), preferred_element_type=F32)


def nn(a, b):
    return lax.dot_general(a, b, (((1,), (0,)), ((), ())), preferred_element_type=F32)


def tn(a, b):
    return lax.dot_general(a, b, (((0,), (0,)), ((), ())), preferred_element_type=F32)


def split3(x):
    hi = x.astype(BF)
    rest = x - hi.astype(F32)
    mid = rest.astype(BF)
    low = (rest - mid.astype(F32)).astype(BF)
    return hi, mid, low


def in_vmem(count):
    return [pl.BlockSpec(memory_space=pltpu.VMEM) for _ in range(count)]


def small(shape, dtype):
    return math.prod(shape) * jnp.dtype(dtype).itemsize <= ON_CHIP_BYTES


def vmem(value):
    if small(value.shape, value.dtype):
        return pltpu.with_memory_space_constraint(value, pltpu.VMEM)
    return value


def held(shape, dtype):
    if small(shape, dtype):
        return pltpu.VMEM(shape, dtype)
    return jax.ShapeDtypeStruct(shape, dtype)


def head_of(h):
    return pl.ds(h * HEAD_DIM, HEAD_DIM)


def pack(block_order, keys, values, queries, grads, outs, sections):
    rows, features = grads.shape
    here = features // sections
    heads = here // HEAD_DIM
    key_count = keys.shape[0]

    def body(order_hbm, k_hbm, v_hbm, q_hbm, g_hbm, o_hbm, *refs):
        blocks = refs[:sections]
        start_ref, k_ref, v_ref, q_ref, g_ref, o_ref, order_ref, sems = refs[sections:]
        pairs = [
            (q_hbm, q_ref),
            (g_hbm, g_ref),
            (o_hbm, o_ref),
            (order_hbm, order_ref),
            (k_hbm, k_ref),
            (v_hbm, v_ref),
        ]
        copies = [pltpu.make_async_copy(*pair, sems.at[i]) for i, pair in enumerate(pairs)]
        for copy in copies:
            copy.start()
        section = lax.axis_index("section")
        lane = lax.broadcasted_iota(jnp.int32, (rows, LANES), 1)

        def at(s, h):
            return pl.ds(pl.multiple_of(s * here + h * HEAD_DIM, HEAD_DIM), HEAD_DIM)

        for i in range(3):
            copies[i].wait()
        for step, out_ref in enumerate(blocks):
            to = section ^ step
            extra = jnp.zeros((rows, LANES), F32)
            for h in range(heads):
                g = g_ref[:, at(to, h)]
                terms = g.astype(F32) * o_ref[:, at(to, h)].astype(F32)
                delta = jnp.sum(terms, axis=1, keepdims=True)
                for part, value in enumerate(split3(delta)):
                    extra = jnp.where(lane == part * heads + h, value.astype(F32), extra)
                out_ref[:, head_of(h)] = q_ref[:, at(to, h)]
                out_ref[:, head_of(heads + 1 + h)] = g
            out_ref[:, head_of(heads)] = extra.astype(BF)
        copies[3].wait()
        block = order_ref[lax.axis_index("ctx")]
        start_ref[...] = jnp.full(start_ref.shape, block * key_count, jnp.int32)
        copies[4].wait()
        copies[5].wait()

    return pl.pallas_call(
        body,
        in_specs=[pl.BlockSpec(memory_space=pl.ANY)] * 6,
        out_specs=in_vmem(sections + 3),
        out_shape=[
            *[held((rows, 2 * here + LANES), BF)] * sections,
            held((8, LANES), jnp.int32),
            held(keys.shape, BF),
            held(values.shape, BF),
        ],
        scratch_shapes=[
            pltpu.VMEM((rows, features), BF),
            pltpu.VMEM((rows, features), BF),
            pltpu.VMEM((rows, features), BF),
            pltpu.SMEM(block_order.shape, jnp.int32),
            pltpu.SemaphoreType.DMA((6,)),
        ],
        name="pack",
    )(block_order, keys, values, queries, grads, outs)


def visible_of(start_ref, shape, row_count, key_total):
    key_pos = start_ref[0:1, 0:1] + lax.broadcasted_iota(jnp.int32, shape, 0)
    row = lax.broadcasted_iota(jnp.int32, shape, 1) % row_count
    return key_pos <= key_total - row_count + row


def stats_kernel(start, queries, keys, row_count, key_total):
    m = queries.shape[0]
    key_count, here = keys.shape
    heads = here // HEAD_DIM
    slots = -(-heads // 8) * 8
    scaling = HEAD_DIM ** (-0.5)

    def body(start_ref, q_ref, k_ref, out_ref, prob_ref, delta_ref, sent_ref):
        visible = visible_of(start_ref, (key_count, m), row_count, key_total)
        out_ref[...] = jnp.ones_like(out_ref)
        for h in range(heads):
            at = head_of(h)
            s = jnp.where(visible, nt(k_ref[:, at], q_ref[:, at]) * scaling, masked_score)
            top = jnp.max(s, axis=0, keepdims=True)
            prob = jnp.where(visible, jnp.exp(s - top), 0.0)
            prob_ref[h] = prob
            out_ref[0, pl.ds(h, 1), :] = top
            out_ref[1, pl.ds(h, 1), :] = jnp.sum(prob, axis=0, keepdims=True)
        slot = lax.broadcasted_iota(jnp.int32, (slots, LANES), 0)
        lane = lax.broadcasted_iota(jnp.int32, (slots, LANES), 1)
        pick = (lane % heads == slot) & (lane < 3 * heads)
        delta_ref[...] = nt(jnp.where(pick, 1.0, 0.0).astype(BF), q_ref[:, pl.ds(here, LANES)])
        sent = jnp.zeros((m, LANES), F32)
        for i in range(2):
            for part, value in enumerate(split3(out_ref[i])):
                at = (3 * i + part) * heads
                place = (lane == at + slot) & (slot < heads)
                sent += tn(value, jnp.where(place, 1.0, 0.0).astype(BF))
        sent_ref[...] = sent.astype(BF)

    return pl.pallas_call(
        body,
        in_specs=in_vmem(3),
        out_specs=in_vmem(4),
        out_shape=[
            held((2, slots, m), F32),
            held((heads, key_count, m), F32),
            held((slots, m), F32),
            held((m, LANES), BF),
        ],
        name="stats",
    )(vmem(start), vmem(queries), vmem(keys))


def query_kernel(grads, keys, values, probs, deltas, sent):
    m = grads.shape[0]
    key_count, here = keys.shape
    heads = here // HEAD_DIM
    scaling = HEAD_DIM ** (-0.5)

    def body(g_ref, k_ref, v_ref, p_ref, d_ref, sent_ref, u_hbm, ds_ref, u_ref, sems):
        def copy_of(h):
            return pltpu.make_async_copy(
                u_ref.at[:, head_of(h)], u_hbm.at[:, head_of(h)], sems.at[h]
            )

        last = pltpu.make_async_copy(sent_ref, u_hbm.at[:, head_of(heads)], sems.at[heads])
        last.start()
        for h in range(heads):
            at = head_of(h)
            ds = p_ref[h] * (nt(v_ref[:, at], g_ref[:, at]) - d_ref[h : h + 1, :]) * scaling
            ds = ds.astype(BF)
            u_ref[:, at] = tn(ds, k_ref[:, at]).astype(BF)
            copy_of(h).start()
            ds_ref[h] = ds
        for h in range(heads):
            copy_of(h).wait()
        last.wait()

    return pl.pallas_call(
        body,
        in_specs=in_vmem(6),
        out_specs=[pl.BlockSpec(memory_space=pl.ANY), in_vmem(1)[0]],
        out_shape=[
            jax.ShapeDtypeStruct((m, here + LANES), BF),
            held((heads, key_count, m), BF),
        ],
        scratch_shapes=[
            pltpu.VMEM((m, here), BF),
            pltpu.SemaphoreType.DMA((heads + 1,)),
        ],
        name="query_gradients",
    )(vmem(grads), vmem(keys), vmem(values), vmem(probs), vmem(deltas), vmem(sent))


def cache_kernel(queries, grads, probs, score_grads, own, merged):
    here = grads.shape[1]
    heads, key_count, _ = probs.shape

    def body(q_ref, g_ref, p_ref, ds_ref, own_ref, all_ref, dk_ref, dv_ref):
        share = jnp.exp(own_ref[0] - all_ref[0]) / all_ref[1]
        for h in range(heads):
            at = head_of(h)
            row = share[h : h + 1, :]
            ds = (ds_ref[h].astype(F32) * row).astype(BF)
            prob = (p_ref[h] * row).astype(BF)
            dk_ref[:, at] = nn(ds, q_ref[:, at]).astype(BF)
            dv_ref[:, at] = nn(prob, g_ref[:, at]).astype(BF)

    return pl.pallas_call(
        body,
        in_specs=in_vmem(6),
        out_specs=in_vmem(2),
        out_shape=[jax.ShapeDtypeStruct((key_count, here), BF)] * 2,
        name="cache_gradients",
    )(vmem(queries), vmem(grads), vmem(probs), vmem(score_grads), vmem(own), vmem(merged))


def combine_kernel(parts):
    sections, holders, rows, width = parts.shape
    here = width - LANES
    heads = here // HEAD_DIM

    def body(p_ref, out_ref):
        def stats_of(s, c):
            e = p_ref[s, c, :, pl.ds(here, LANES)].astype(F32)
            e += pltpu.roll(e, LANES - heads, 1) + pltpu.roll(e, LANES - 2 * heads, 1)
            return e, pltpu.roll(e, LANES - 3 * heads, 1)

        for s in range(sections):
            top = jnp.full((rows, LANES), -jnp.inf, F32)
            for c in range(holders):
                top = jnp.maximum(top, stats_of(s, c)[0])
            total = jnp.zeros((rows, LANES), F32)
            for c in range(holders):
                own, count = stats_of(s, c)
                total += jnp.exp(own - top) * count
            sums = [jnp.zeros((rows, HEAD_DIM), F32) for _ in range(heads)]
            for c in range(holders):
                share = jnp.exp(stats_of(s, c)[0] - top) / total
                for h in range(heads):
                    value = p_ref[s, c, :, head_of(h)].astype(F32)
                    sums[h] += share[:, h : h + 1] * value
            for h in range(heads):
                out_ref[:, head_of(s * heads + h)] = sums[h].astype(BF)

    return pl.pallas_call(
        body,
        in_specs=in_vmem(1),
        out_specs=in_vmem(1)[0],
        out_shape=jax.ShapeDtypeStruct((rows, sections * here), BF),
        name="combine",
    )(vmem(parts))


def merge_stats(stats, axis, order):
    for bit in order:
        other = flip(stats, axis, 1 << bit)
        top = jnp.maximum(stats[0], other[0])
        total = stats[1] * jnp.exp(stats[0] - top) + other[1] * jnp.exp(other[0] - top)
        stats = jnp.stack([top, total])
    return stats


def flip(value, axis, bit):
    count = lax.axis_size(axis)
    return lax.ppermute(value, axis, [(i, i ^ bit) for i in range(count)])


def ordered(mine, other, upper, axis):
    first = jnp.where(upper, other, mine)
    second = jnp.where(upper, mine, other)
    return jnp.stack([first, second], axis)


def swap_blocks(blocks, axis):
    count = lax.axis_size(axis)
    here = lax.axis_index(axis)
    got = [blocks[0]]
    for step in range(1, count):
        got.append(flip(blocks[step], axis, step))
    bit = 1
    while bit < count:
        upper = here & bit != 0
        got = [jnp.where(upper, got[i ^ bit], got[i]) for i in range(count)]
        bit *= 2
    return jnp.stack(got)


def spread_blocks(blocks, axis, order):
    count = lax.axis_size(axis)
    lead, rest = blocks.shape[0], blocks.shape[1:]
    done = []
    for bit in order:
        upper = lax.axis_index(axis) & (1 << bit) != 0
        other = flip(blocks, axis, 1 << bit)
        blocks = ordered(blocks, other, upper, 1 + sum(b > bit for b in done))
        done.append(bit)
    return blocks.reshape((lead, count) + rest)


def exchange(blocks):
    return lax.all_to_all(blocks, ("section", "ctx"), 0, 0, tiled=True)


def compute(block_order, queries, cache_keys, cache_values, attention_out, output_grad):
    sections = lax.axis_size("section")
    ctx_count = lax.axis_size("ctx")
    assert ctx_count & (ctx_count - 1) == 0
    assert sections & (sections - 1) == 0 and sections > 1
    layers, rows, _ = queries.shape
    assert layers == 1
    key_count, here = cache_keys.shape
    row_count = rows * ctx_count
    key_total = key_count * ctx_count
    peers = sections * ctx_count

    ctx_bits = ctx_count.bit_length() - 1
    down = list(range(ctx_bits))[::-1]

    packed = pack(
        block_order,
        cache_keys,
        cache_values,
        queries[0],
        output_grad[0],
        attention_out[0],
        sections,
    )
    start, keys, values = packed[sections:]
    swapped = swap_blocks(packed[:sections], "section")
    query_all, grad_all = swapped[..., : here + LANES], swapped[..., here + LANES :]
    query_all = spread_blocks(query_all, "ctx", down)
    query_all = query_all.reshape(peers * rows, here + LANES)
    grad_all = spread_blocks(grad_all, "ctx", down[:1] + down[1:][::-1])
    grad_all = grad_all.reshape(peers * rows, here)

    own, probs, deltas, row_stats = stats_kernel(start, query_all, keys, row_count, key_total)
    merged = merge_stats(own, "ctx", down[-1:] + down[:-1])
    part, score_grads = query_kernel(grad_all, keys, values, probs, deltas, row_stats)
    part = exchange(part.reshape(peers, rows, here + LANES))
    grad_keys, grad_values = cache_kernel(query_all, grad_all, probs, score_grads, own, merged)
    grad_queries = combine_kernel(part.reshape(sections, ctx_count, rows, here + LANES))
    return (grad_queries[None], grad_keys, grad_values)


def solution(mesh):
    in_specs = (
        P(),
        P("section", "ctx", None),
        P("ctx", "section"),
        P("ctx", "section"),
        P("section", "ctx", None),
        P("section", "ctx", None),
    )
    out_specs = (P("section", "ctx", None), P("ctx", "section"), P("ctx", "section"))
    return jax.shard_map(compute, mesh=mesh, in_specs=in_specs, out_specs=out_specs, check_vma=False)
```

profile of v0, /device:TPU:0, one launch (start us, length us, event | category | flops | bytes accessed | tf_op | source)
XLA Modules:
  0.0 54.1 jit_solution(6744622742947326622)
XLA Ops:
  0.6 1.1 %pack.1 = (bf16[8,1408]{1,0:T(8,128)(2,1)S(1)}, bf16[8,1408]{1,0:T(8,128)(2,1)S(1)}, bf16[8,1408]{1,0:T(8,128)(2,1)S(1)}, bf16[8,1408]{1,0:T(8,128)(2,1)S(1)}, s...) custom-call(s32[8]{0:T(128)} %order_hbm.1, bf16[128,640]{1,0:T(8,128)(2,1)} %k_hbm.1, ...), custom_call_target="tpu_custom_call" | custom-call | tf_op jit(solution)/shard_map/pack/pallas_call | solution.py:109
  1.8 2.5 %collective-permute-start = (bf16[8,1408]{1,0:T(8,128)(2,1)S(1)}, bf16[8,1408]{1,0:T(8,128)(2,1)S(1)}, u32[]{:S(2)}, u32[]{:S(2)}) collective-permute-start(bf16[8,1408]{1,0:T(8,128)(2,1)S(1)} %get-tuple-element.18), channel_id=1, source_target_pairs={{0,24},{8,16},{16,8},{24,0},{1,25},{9,17},{17,9},{25,1},{2,26},{10... | collective-permute-start | bytes 67592 | tf_op jit(solution)/shard_map/ppermute | solution.py:292
  4.2 0.6 %collective-permute-start.1 = (bf16[8,1408]{1,0:T(8,128)(2,1)S(1)}, bf16[8,1408]{1,0:T(8,128)(2,1)S(1)}, u32[]{:S(2)}, u32[]{:S(2)}) collective-permute-start(bf16[8,1408]{1,0:T(8,128)(2,1)S(1)} %get-tuple-element.19), channel_id=1, source_target_pairs={{0,16},{8,24},{16,0},{24,8},{1,17},{9,25},{17,1},{25,9},{2,18},{10... | collective-permute-start | bytes 67592 | tf_op jit(solution)/shard_map/ppermute | solution.py:292
  4.9 0.9 %collective-permute-done = bf16[8,1408]{1,0:T(8,128)(2,1)S(1)} collective-permute-done((bf16[8,1408]{1,0:T(8,128)(2,1)S(1)}, bf16[8,1408]{1,0:T(8,128)(2,1)S(1)}, u32[]{:S(2)}, u32[]{:S(2)}) %collective-permute-start) | collective-permute-done | bytes 22560 | tf_op jit(solution)/shard_map/ppermute | solution.py:292
  5.8 2.2 %collective-permute-done.1 = bf16[8,1408]{1,0:T(8,128)(2,1)S(1)} collective-permute-done((bf16[8,1408]{1,0:T(8,128)(2,1)S(1)}, bf16[8,1408]{1,0:T(8,128)(2,1)S(1)}, u32[]{:S(2)}, u32[]{:S(2)}) %collective-permute-start.1) | collective-permute-done | bytes 22560 | tf_op jit(solution)/shard_map/ppermute | solution.py:292
  8.1 2.7 %collective-permute-start.3 = (bf16[4,8,640]{2,1,0:T(8,128)(2,1)S(1)}, bf16[4,8,640]{2,1,0:T(8,128)(2,1)S(1)}, u32[]{:S(2)}, u32[]{:S(2)}) collective-permute-start(bf16[4,8,640]{2,1,0:T(8,128)(2,1)S(1)} %pad_maximum_fusion.9), channel_id=1, source_target_pairs={{0,4},{1,5},{2,6},{3,7},{4,0},{5,1},{6,2},{7,3},{8,12},{9,13},{10,... | collective-permute-start | bytes 122888 | tf_op jit(solution)/shard_map/ppermute | solution.py:292
  11.1 2.0 %collective-permute-done.3 = bf16[4,8,640]{2,1,0:T(8,128)(2,1)S(1)} collective-permute-done((bf16[4,8,640]{2,1,0:T(8,128)(2,1)S(1)}, bf16[4,8,640]{2,1,0:T(8,128)(2,1)S(1)}, u32[]{:S(2)}, u32[]{:S(2)}) %collective-permute-start.3) | collective-permute-done | bytes 40992 | tf_op jit(solution)/shard_map/ppermute | solution.py:292
  13.1 1.6 %collective-permute-start.4 = (bf16[4,2,8,640]{3,2,0,1:T(8,128)(2,1)S(1)}, bf16[4,2,8,640]{3,2,0,1:T(8,128)(2,1)S(1)}, u32[]{:S(2)}, u32[]{:S(2)}) collective-permute-start(bf16[4,2,8,640]{3,2,0,1:T(8,128)(2,1)S(1)} %pad_maximum_fusion.5), channel_id=1, source_target_pairs={{0,1},{1,0},{2,3},{3,2},{4,5},{5,4},{6,7},{7,6},{8,9},{9,8},{10,11... | collective-permute-start | bytes 245768 | tf_op jit(solution)/shard_map/ppermute | solution.py:292
  14.7 1.0 %collective-permute-done.6 = bf16[4,8,768]{2,1,0:T(8,128)(2,1)S(1)} collective-permute-done((bf16[4,8,768]{2,1,0:T(8,128)(2,1)S(1)}, bf16[4,8,768]{2,1,0:T(8,128)(2,1)S(1)}, u32[]{:S(2)}, u32[]{:S(2)}) %collective-permute-start.6) | collective-permute-done | bytes 49184 | tf_op jit(solution)/shard_map/ppermute | solution.py:292
  15.8 1.6 %collective-permute-start.7 = (bf16[4,2,8,768]{3,2,0,1:T(8,128)(2,1)S(1)}, bf16[4,2,8,768]{3,2,0,1:T(8,128)(2,1)S(1)}, u32[]{:S(2)}, u32[]{:S(2)}) collective-permute-start(bf16[4,2,8,768]{3,2,0,1:T(8,128)(2,1)S(1)} %pad_maximum_fusion.4), channel_id=1, source_target_pairs={{0,2},{1,3},{2,0},{3,1},{4,6},{5,7},{6,4},{7,5},{8,10},{9,11},{10,... | collective-permute-start | bytes 294920 | tf_op jit(solution)/shard_map/ppermute | solution.py:292
  17.7 2.1 %collective-permute-start.5 = (bf16[4,2,2,8,640]{4,3,0,1,2:T(8,128)(2,1)S(1)}, bf16[4,2,2,8,640]{4,3,0,1,2:T(8,128)(2,1)S(1)}, u32[]{:S(2)}, u32[]{:S(2)}) collective-permute-start(bf16[4,2,2,8,640]{4,3,0,1,2:T(8,128)(2,1)S(1)} %pad_maximum_fusion.3), channel_id=1, source_target_pairs={{0,2},{1,3},{2,0},{3,1},{4,6},{5,7},{6,4},{7,5},{8,10},{9,11},{10,... | collective-permute-start | bytes 491528 | tf_op jit(solution)/shard_map/ppermute | solution.py:292
  19.8 1.0 %collective-permute-done.7 = bf16[4,2,8,768]{3,2,0,1:T(8,128)(2,1)S(1)} collective-permute-done((bf16[4,2,8,768]{3,2,0,1:T(8,128)(2,1)S(1)}, bf16[4,2,8,768]{3,2,0,1:T(8,128)(2,1)S(1)}, u32[]{:S(2)}, u32[]{:S(2)}) %collective-permute-start.7) | collective-permute-done | bytes 98336 | tf_op jit(solution)/shard_map/ppermute | solution.py:292
  20.9 1.6 %collective-permute-start.8 = (bf16[4,2,2,8,768]{4,3,0,1,2:T(8,128)(2,1)S(1)}, bf16[4,2,2,8,768]{4,3,0,1,2:T(8,128)(2,1)S(1)}, u32[]{:S(2)}, u32[]{:S(2)}) collective-permute-start(bf16[4,2,2,8,768]{4,3,0,1,2:T(8,128)(2,1)S(1)} %pad_maximum_fusion.2), channel_id=1, source_target_pairs={{0,1},{1,0},{2,3},{3,2},{4,5},{5,4},{6,7},{7,6},{8,9},{9,8},{10,11... | collective-permute-start | bytes 589832 | tf_op jit(solution)/shard_map/ppermute | solution.py:292
  22.5 0.6 %collective-permute-done.5 = bf16[4,2,2,8,640]{4,3,0,1,2:T(8,128)(2,1)S(1)} collective-permute-done((bf16[4,2,2,8,640]{4,3,0,1,2:T(8,128)(2,1)S(1)}, bf16[4,2,2,8,640]{4,3,0,1,2:T(8,128)(2,1)S(1)}, u32[]{:S(2)}, u32[]{:S(2)}) %collective-permute-start.5) | collective-permute-done | bytes 163872 | tf_op jit(solution)/shard_map/ppermute | solution.py:292
  23.1 3.7 %collective-permute-done.8 = bf16[4,2,2,8,768]{4,3,0,1,2:T(8,128)(2,1)S(1)} collective-permute-done((bf16[4,2,2,8,768]{4,3,0,1,2:T(8,128)(2,1)S(1)}, bf16[4,2,2,8,768]{4,3,0,1,2:T(8,128)(2,1)S(1)}, u32[]{:S(2)}, u32[]{:S(2)}) %collective-permute-start.8) | collective-permute-done | bytes 196640 | tf_op jit(solution)/shard_map/ppermute | solution.py:292
  26.9 0.8 %stats.1 = (f32[2,8,256]{2,1,0:T(8,128)S(1)}, f32[5,128,256]{2,1,0:T(8,128)S(1)}, f32[8,256]{1,0:T(8,128)S(1)}, bf16[256,128]{1,0:T(8,128)(2,1)S(1)}) custom-call(s32[8,128]{1,0:T(8,128)S(1)} %get-tuple-element.24.start_ref, bf16[256,768]{1,0:T(8,128)(2,1)S(1)} %bitcast.40, bf16[128,640]{1,0:T(8,128)(2,1)S(1)} %get-tuple-element.22.k_ref), custom_call_target="tpu_custom_call" | custom-call | tf_op jit(solution)/shard_map/stats/pallas_call | solution.py:166
  27.7 1.6 %collective-permute-start.9 = (f32[2,8,256]{2,1,0:T(8,128)S(1)}, f32[2,8,256]{2,1,0:T(8,128)S(1)}, u32[]{:S(2)}, u32[]{:S(2)}) collective-permute-start(f32[2,8,256]{2,1,0:T(8,128)S(1)} %get-tuple-element.30.own_ref), channel_id=1, source_target_pairs={{0,1},{1,0},{2,3},{3,2},{4,5},{5,4},{6,7},{7,6},{8,9},{9,8},{10,11... | collective-permute-start | bytes 49160 | tf_op jit(solution)/shard_map/ppermute | solution.py:292
  29.4 1.4 %query_gradients.1 = (bf16[256,768]{1,0:T(8,128)(2,1)}, bf16[5,128,256]{2,1,0:T(8,128)(2,1)S(1)}) custom-call(bf16[256,640]{1,0:T(8,128)(2,1)S(1)} %bitcast.42, bf16[128,640]{1,0:T(8,128)(2,1)S(1)} %get-tuple-element.22.k_ref, bf16[128,640]{1,0:T(8,128)(2,1)S(1)} %get-tuple-element.23.v_ref, f32[5,128,256]{2,1,0:T(8,128)S(1)} %get-tuple-element.25.p_ref, ...), custom_call_target="tpu_custom_call" | custom-call | tf_op jit(solution)/shard_map/query_gradients/pallas_call | solution.py:205
  30.8 4.2 %all-to-all-start = ((bf16[32,8,768]{2,1,0:T(8,128)(2,1)}), bf16[32,8,768]{2,1,0:T(8,128)(2,1)S(1)}, u32[]{:S(2)}, u32[]{:S(2)}) async-start(bf16[32,8,768]{2,1,0:T(8,128)(2,1)} %bitcast.45), calls=%async_computation | async-start | bytes 786432 | tf_op jit(solution)/shard_map/all_to_all | solution.py:328
  35.0 2.7 %collective-permute-start.10 = (f32[2,8,256]{2,1,0:T(8,128)S(1)}, f32[2,8,256]{2,1,0:T(8,128)S(1)}, u32[]{:S(2)}, u32[]{:S(2)}) collective-permute-start(f32[2,8,256]{2,1,0:T(8,128)S(1)} %pad_maximum_fusion.10), channel_id=1, source_target_pairs={{0,4},{1,5},{2,6},{3,7},{4,0},{5,1},{6,2},{7,3},{8,12},{9,13},{10,... | collective-permute-start | bytes 49160 | tf_op jit(solution)/shard_map/ppermute | solution.py:292
  37.7 10.1 %collective-permute-done.10 = f32[2,8,256]{2,1,0:T(8,128)S(1)} collective-permute-done((f32[2,8,256]{2,1,0:T(8,128)S(1)}, f32[2,8,256]{2,1,0:T(8,128)S(1)}, u32[]{:S(2)}, u32[]{:S(2)}) %collective-permute-start.10) | collective-permute-done | bytes 16416 | tf_op jit(solution)/shard_map/ppermute | solution.py:292
  47.9 3.7 %collective-permute-done.11 = f32[2,8,256]{2,1,0:T(8,128)S(1)} collective-permute-done((f32[2,8,256]{2,1,0:T(8,128)S(1)}, f32[2,8,256]{2,1,0:T(8,128)S(1)}, u32[]{:S(2)}, u32[]{:S(2)}) %collective-permute-start.11) | collective-permute-done | bytes 16416 | tf_op jit(solution)/shard_map/ppermute | solution.py:292
  51.7 1.0 %cache_gradients.1 = (bf16[128,640]{1,0:T(8,128)(2,1)}, bf16[128,640]{1,0:T(8,128)(2,1)}) custom-call(bf16[256,768]{1,0:T(8,128)(2,1)S(1)} %bitcast.41, bf16[256,640]{1,0:T(8,128)(2,1)S(1)} %bitcast.43, f32[5,128,256]{2,1,0:T(8,128)S(1)} %get-tuple-element.25.p_ref, bf16[5,128,256]{2,1,0:T(8,128)(2,1)S(1)} %get-tuple-element.29.ds_ref, ...), custom_call_target="tpu_custom_call" | custom-call | tf_op jit(solution)/shard_map/cache_gradients/pallas_call | solution.py:235
  52.7 1.4 %combine.1 = bf16[8,2560]{1,0:T(8,128)(2,1)} custom-call(bf16[4,8,8,768]{3,2,1,0:T(8,128)(2,1)S(1)} %bitcast.44), custom_call_target="tpu_custom_call" | custom-call | tf_op jit(solution)/shard_map/combine/pallas_call | solution.py:272
  (30 shorter events, 1.1 us)
Async XLA Ops:
  1.8 4.0 %collective-permute-start = (bf16[8,1408]{1,0:T(8,128)(2,1)S(1)}, bf16[8,1408]{1,0:T(8,128)(2,1)S(1)}, u32[]{:S(2)}, u32[]{:S(2)}) collective-permute-start(bf16[8,1408]{1,0:T(8,128)(2,1)S(1)} %get-tuple-element.18), channel_id=1, source_target_pairs={{0,24},{8,16},{16,8},{24,0},{1,25},{9,17},{17,9},{25,1},{2,26},{10... | collective-permute-start | bytes 67592 | tf_op jit(solution)/shard_map/ppermute | solution.py:292
  4.2 3.8 %collective-permute-start.1 = (bf16[8,1408]{1,0:T(8,128)(2,1)S(1)}, bf16[8,1408]{1,0:T(8,128)(2,1)S(1)}, u32[]{:S(2)}, u32[]{:S(2)}) collective-permute-start(bf16[8,1408]{1,0:T(8,128)(2,1)S(1)} %get-tuple-element.19), channel_id=1, source_target_pairs={{0,16},{8,24},{16,0},{24,8},{1,17},{9,25},{17,1},{25,9},{2,18},{10... | collective-permute-start | bytes 67592 | tf_op jit(solution)/shard_map/ppermute | solution.py:292
  4.9 3.2 %collective-permute-start.2 = (bf16[8,1408]{1,0:T(8,128)(2,1)S(1)}, bf16[8,1408]{1,0:T(8,128)(2,1)S(1)}, u32[]{:S(2)}, u32[]{:S(2)}) collective-permute-start(bf16[8,1408]{1,0:T(8,128)(2,1)S(1)} %get-tuple-element.20), channel_id=1, source_target_pairs={{0,8},{8,0},{16,24},{24,16},{1,9},{9,1},{17,25},{25,17},{2,10},{10... | collective-permute-start | bytes 67592 | tf_op jit(solution)/shard_map/ppermute | solution.py:292
  8.1 5.0 %collective-permute-start.3 = (bf16[4,8,640]{2,1,0:T(8,128)(2,1)S(1)}, bf16[4,8,640]{2,1,0:T(8,128)(2,1)S(1)}, u32[]{:S(2)}, u32[]{:S(2)}) collective-permute-start(bf16[4,8,640]{2,1,0:T(8,128)(2,1)S(1)} %pad_maximum_fusion.9), channel_id=1, source_target_pairs={{0,4},{1,5},{2,6},{3,7},{4,0},{5,1},{6,2},{7,3},{8,12},{9,13},{10,... | collective-permute-start | bytes 122888 | tf_op jit(solution)/shard_map/ppermute | solution.py:292
  10.7 5.0 %collective-permute-start.6 = (bf16[4,8,768]{2,1,0:T(8,128)(2,1)S(1)}, bf16[4,8,768]{2,1,0:T(8,128)(2,1)S(1)}, u32[]{:S(2)}, u32[]{:S(2)}) collective-permute-start(bf16[4,8,768]{2,1,0:T(8,128)(2,1)S(1)} %pad_maximum_fusion.6), channel_id=1, source_target_pairs={{0,4},{1,5},{2,6},{3,7},{4,0},{5,1},{6,2},{7,3},{8,12},{9,13},{10,... | collective-permute-start | bytes 147464 | tf_op jit(solution)/shard_map/ppermute | solution.py:292
  13.1 4.5 %collective-permute-start.4 = (bf16[4,2,8,640]{3,2,0,1:T(8,128)(2,1)S(1)}, bf16[4,2,8,640]{3,2,0,1:T(8,128)(2,1)S(1)}, u32[]{:S(2)}, u32[]{:S(2)}) collective-permute-start(bf16[4,2,8,640]{3,2,0,1:T(8,128)(2,1)S(1)} %pad_maximum_fusion.5), channel_id=1, source_target_pairs={{0,1},{1,0},{2,3},{3,2},{4,5},{5,4},{6,7},{7,6},{8,9},{9,8},{10,11... | collective-permute-start | bytes 245768 | tf_op jit(solution)/shard_map/ppermute | solution.py:292
  15.8 5.1 %collective-permute-start.7 = (bf16[4,2,8,768]{3,2,0,1:T(8,128)(2,1)S(1)}, bf16[4,2,8,768]{3,2,0,1:T(8,128)(2,1)S(1)}, u32[]{:S(2)}, u32[]{:S(2)}) collective-permute-start(bf16[4,2,8,768]{3,2,0,1:T(8,128)(2,1)S(1)} %pad_maximum_fusion.4), channel_id=1, source_target_pairs={{0,2},{1,3},{2,0},{3,1},{4,6},{5,7},{6,4},{7,5},{8,10},{9,11},{10,... | collective-permute-start | bytes 294920 | tf_op jit(solution)/shard_map/ppermute | solution.py:292
  17.7 5.4 %collective-permute-start.5 = (bf16[4,2,2,8,640]{4,3,0,1,2:T(8,128)(2,1)S(1)}, bf16[4,2,2,8,640]{4,3,0,1,2:T(8,128)(2,1)S(1)}, u32[]{:S(2)}, u32[]{:S(2)}) collective-permute-start(bf16[4,2,2,8,640]{4,3,0,1,2:T(8,128)(2,1)S(1)} %pad_maximum_fusion.3), channel_id=1, source_target_pairs={{0,2},{1,3},{2,0},{3,1},{4,6},{5,7},{6,4},{7,5},{8,10},{9,11},{10,... | collective-permute-start | bytes 491528 | tf_op jit(solution)/shard_map/ppermute | solution.py:292
  20.9 5.9 %collective-permute-start.8 = (bf16[4,2,2,8,768]{4,3,0,1,2:T(8,128)(2,1)S(1)}, bf16[4,2,2,8,768]{4,3,0,1,2:T(8,128)(2,1)S(1)}, u32[]{:S(2)}, u32[]{:S(2)}) collective-permute-start(bf16[4,2,2,8,768]{4,3,0,1,2:T(8,128)(2,1)S(1)} %pad_maximum_fusion.2), channel_id=1, source_target_pairs={{0,1},{1,0},{2,3},{3,2},{4,5},{5,4},{6,7},{7,6},{8,9},{9,8},{10,11... | collective-permute-start | bytes 589832 | tf_op jit(solution)/shard_map/ppermute | solution.py:292
  27.7 7.3 %collective-permute-start.9 = (f32[2,8,256]{2,1,0:T(8,128)S(1)}, f32[2,8,256]{2,1,0:T(8,128)S(1)}, u32[]{:S(2)}, u32[]{:S(2)}) collective-permute-start(f32[2,8,256]{2,1,0:T(8,128)S(1)} %get-tuple-element.30.own_ref), channel_id=1, source_target_pairs={{0,1},{1,0},{2,3},{3,2},{4,5},{5,4},{6,7},{7,6},{8,9},{9,8},{10,11... | collective-permute-start | bytes 49160 | tf_op jit(solution)/shard_map/ppermute | solution.py:292
  30.8 22.0 %all-to-all-start = ((bf16[32,8,768]{2,1,0:T(8,128)(2,1)}), bf16[32,8,768]{2,1,0:T(8,128)(2,1)S(1)}, u32[]{:S(2)}, u32[]{:S(2)}) async-start(bf16[32,8,768]{2,1,0:T(8,128)(2,1)} %bitcast.45), calls=%async_computation | async-start | bytes 786432 | tf_op jit(solution)/shard_map/all_to_all | solution.py:328
  35.0 12.8 %collective-permute-start.10 = (f32[2,8,256]{2,1,0:T(8,128)S(1)}, f32[2,8,256]{2,1,0:T(8,128)S(1)}, u32[]{:S(2)}, u32[]{:S(2)}) collective-permute-start(f32[2,8,256]{2,1,0:T(8,128)S(1)} %pad_maximum_fusion.10), channel_id=1, source_target_pairs={{0,4},{1,5},{2,6},{3,7},{4,0},{5,1},{6,2},{7,3},{8,12},{9,13},{10,... | collective-permute-start | bytes 49160 | tf_op jit(solution)/shard_map/ppermute | solution.py:292
  47.9 3.8 %collective-permute-start.11 = (f32[2,8,256]{2,1,0:T(8,128)S(1)}, f32[2,8,256]{2,1,0:T(8,128)S(1)}, u32[]{:S(2)}, u32[]{:S(2)}) collective-permute-start(f32[2,8,256]{2,1,0:T(8,128)S(1)} %pad_maximum_fusion.11), channel_id=1, source_target_pairs={{0,2},{1,3},{2,0},{3,1},{4,6},{5,7},{6,4},{7,5},{8,10},{9,11},{10,... | collective-permute-start | bytes 49160 | tf_op jit(solution)/shard_map/ppermute | solution.py:292
where the time goes:
time: 54.4 us; the launch traced here: 54.1 us
  waiting for transfers between devices  25.5 us (47%)
  starting transfers between devices  21.7 us (40%)
  Pallas kernels  5.72 us (11%)
  between operations  0.82 us (2%)
    ppermute x12, waiting for transfers between devices, flip(): return lax.ppermute(value, axis, [(i, i ^ bit) for i in range(count)])  25.5 us
    ppermute x12, starting transfers between devices, flip(): return lax.ppermute(value, axis, [(i, i ^ bit) for i in range(count)])  17.5 us
    all_to_all x1, starting transfers between devices, exchange(): return lax.all_to_all(blocks, ('section', 'ctx'), 0, 0, tiled=True)  4.19 us
    pallas_call x1, Pallas kernels, query_kernel(): pl.pallas_call(body, in_specs=in_vmem(6), out_specs=[pl.BlockSpec(memory_...  1.41 us
    pallas_call x1, Pallas kernels, combine_kernel(): pl.pallas_call(body, in_specs=in_vmem(1), out_specs=in_vmem(1)[0], out_sh...  1.37 us
    pallas_call x1, Pallas kernels, pack(): pl.pallas_call(body, in_specs=[pl.BlockSpec(memory_space=pl.ANY)] * 6, ou...  1.12 us
  transfers between devices with their start and end apart: 13, of which 10 were waited for; matrix products, arithmetic and copies ran while one was open for 1% of the time, Pallas kernels for 5%

commit v1 on v0

--- a/solution.py
+++ b/solution.py
@@ -312,15 +312,28 @@
     return jnp.stack(got)
 
 
-def spread_blocks(blocks, axis, order):
-    count = lax.axis_size(axis)
+def flip_by_parity(value, bits):
+    sections, count = lax.axis_size("section"), lax.axis_size("ctx")
+    pairs = []
+    for section in range(sections):
+        for at in range(count):
+            to = at ^ (1 << bits[section % 2])
+            pairs.append((section * count + at, section * count + to))
+    return lax.ppermute(value, ("section", "ctx"), pairs)
+
+
+def spread_blocks(blocks, first_bits, last_bits):
+    count = lax.axis_size("ctx")
+    at = lax.axis_index("ctx")
+    odd = lax.axis_index("section") % 2 == 1
     lead, rest = blocks.shape[0], blocks.shape[1:]
-    done = []
-    for bit in order:
-        upper = lax.axis_index(axis) & (1 << bit) != 0
-        other = flip(blocks, axis, 1 << bit)
-        blocks = ordered(blocks, other, upper, 1 + sum(b > bit for b in done))
-        done.append(bit)
+    pairs = [(bit, bit) for bit in first_bits] + [last_bits, last_bits[::-1]]
+    for i, (even_bit, odd_bit) in enumerate(pairs):
+        upper = at >> jnp.where(odd, odd_bit, even_bit) & 1 == 1
+        other = flip_by_parity(blocks, (even_bit, odd_bit))
+        blocks = ordered(blocks, other, upper, 1 + i)
+    turned = odd if last_bits[0] > last_bits[1] else ~odd
+    blocks = jnp.where(turned, jnp.swapaxes(blocks, i, i + 1), blocks)
     return blocks.reshape((lead, count) + rest)
 
 
@@ -331,7 +344,7 @@
 def compute(block_order, queries, cache_keys, cache_values, attention_out, output_grad):
     sections = lax.axis_size("section")
     ctx_count = lax.axis_size("ctx")
-    assert ctx_count & (ctx_count - 1) == 0
+    assert ctx_count & (ctx_count - 1) == 0 and ctx_count > 2
     assert sections & (sections - 1) == 0 and sections > 1
     layers, rows, _ = queries.shape
     assert layers == 1
@@ -355,9 +368,10 @@
     start, keys, values = packed[sections:]
     swapped = swap_blocks(packed[:sections], "section")
     query_all, grad_all = swapped[..., : here + LANES], swapped[..., here + LANES :]
-    query_all = spread_blocks(query_all, "ctx", down)
+    last = (down[-2], down[-1])
+    query_all = spread_blocks(query_all, down[:-2], last)
     query_all = query_all.reshape(peers * rows, here + LANES)
-    grad_all = spread_blocks(grad_all, "ctx", down[:1] + down[1:][::-1])
+    grad_all = spread_blocks(grad_all, down[:-2], last[::-1])
     grad_all = grad_all.reshape(peers * rows, here)
 
     own, probs, deltas, row_stats = stats_kernel(start, query_all, keys, row_count, key_total)

time: 54.4 us -> 54.3 us (level)
    ppermute x12 -> x6, starting transfers between devices: 17.5 us -> 7.54 us  [flip(): return lax.ppermute(value, axis, [(i, i ^ bit) for i in range(count)])]
    ppermute x0 -> x6, starting transfers between devices: none -> 9.83 us  [flip_by_parity(): return lax.ppermute(value, ('section', 'ctx'), pairs)]
    ppermute x12 -> x6, waiting for transfers between devices: 25.5 us -> 16.9 us  [flip(): return lax.ppermute(value, axis, [(i, i ^ bit) for i in range(count)])]
    ppermute x0 -> x6, waiting for transfers between devices: none -> 8.14 us  [flip_by_parity(): return lax.ppermute(value, ('section', 'ctx'), pairs)]
where the time goes in v1:
time: 54.3 us; the launch traced here: 54 us
  waiting for transfers between devices  25.1 us (46%)
  starting transfers between devices  21.9 us (40%)
  Pallas kernels  5.72 us (11%)
  between operations  0.83 us (2%)
    ppermute x6, waiting for transfers between devices, flip(): return lax.ppermute(value, axis, [(i, i ^ bit) for i in range(count)])  16.9 us
    ppermute x6, starting transfers between devices, flip_by_parity(): return lax.ppermute(value, ('section', 'ctx'), pairs)  9.83 us
    ppermute x6, waiting for transfers between devices, flip_by_parity(): return lax.ppermute(value, ('section', 'ctx'), pairs)  8.14 us
    ppermute x6, starting transfers between devices, flip(): return lax.ppermute(value, axis, [(i, i ^ bit) for i in range(count)])  7.54 us
    all_to_all x1, starting transfers between devices, exchange(): return lax.all_to_all(blocks, ('section', 'ctx'), 0, 0, tiled=True)  4.54 us
    pallas_call x1, Pallas kernels, query_kernel(): pl.pallas_call(body, in_specs=in_vmem(6), out_specs=[pl.BlockSpec(memory_...  1.41 us
    pallas_call x1, Pallas kernels, combine_kernel(): pl.pallas_call(body, in_specs=in_vmem(1), out_specs=in_vmem(1)[0], out_sh...  1.37 us
    pallas_call x1, Pallas kernels, pack(): pl.pallas_call(body, in_specs=[pl.BlockSpec(memory_space=pl.ANY)] * 6, ou...  1.12 us
  transfers between devices with their start and end apart: 13, of which 10 were waited for; matrix products, arithmetic and copies ran while one was open for 1% of the time, Pallas kernels for 5%

profile of v1, /device:TPU:0, one launch (start us, length us, event | category | flops | bytes accessed | tf_op | source)
XLA Modules:
  0.0 54.0 jit_solution(16759460355283840893)
XLA Ops:
  0.6 1.1 %pack.1 = (bf16[8,1408]{1,0:T(8,128)(2,1)S(1)}, bf16[8,1408]{1,0:T(8,128)(2,1)S(1)}, bf16[8,1408]{1,0:T(8,128)(2,1)S(1)}, bf16[8,1408]{1,0:T(8,128)(2,1)S(1)}, s...) custom-call(s32[8]{0:T(128)} %order_hbm.1, bf16[128,640]{1,0:T(8,128)(2,1)} %k_hbm.1, ...), custom_call_target="tpu_custom_call" | custom-call | tf_op jit(solution)/shard_map/pack/pallas_call | solution.py:109
  1.8 2.5 %collective-permute-start = (bf16[8,1408]{1,0:T(8,128)(2,1)S(1)}, bf16[8,1408]{1,0:T(8,128)(2,1)S(1)}, u32[]{:S(2)}, u32[]{:S(2)}) collective-permute-start(bf16[8,1408]{1,0:T(8,128)(2,1)S(1)} %get-tuple-element.18), channel_id=1, source_target_pairs={{0,24},{8,16},{16,8},{24,0},{1,25},{9,17},{17,9},{25,1},{2,26},{10... | collective-permute-start | bytes 67592 | tf_op jit(solution)/shard_map/ppermute | solution.py:292
  4.2 0.6 %collective-permute-start.1 = (bf16[8,1408]{1,0:T(8,128)(2,1)S(1)}, bf16[8,1408]{1,0:T(8,128)(2,1)S(1)}, u32[]{:S(2)}, u32[]{:S(2)}) collective-permute-start(bf16[8,1408]{1,0:T(8,128)(2,1)S(1)} %get-tuple-element.19), channel_id=1, source_target_pairs={{0,16},{8,24},{16,0},{24,8},{1,17},{9,25},{17,1},{25,9},{2,18},{10... | collective-permute-start | bytes 67592 | tf_op jit(solution)/shard_map/ppermute | solution.py:292
  4.9 0.9 %collective-permute-done = bf16[8,1408]{1,0:T(8,128)(2,1)S(1)} collective-permute-done((bf16[8,1408]{1,0:T(8,128)(2,1)S(1)}, bf16[8,1408]{1,0:T(8,128)(2,1)S(1)}, u32[]{:S(2)}, u32[]{:S(2)}) %collective-permute-start) | collective-permute-done | bytes 22560 | tf_op jit(solution)/shard_map/ppermute | solution.py:292
  5.8 2.2 %collective-permute-done.1 = bf16[8,1408]{1,0:T(8,128)(2,1)S(1)} collective-permute-done((bf16[8,1408]{1,0:T(8,128)(2,1)S(1)}, bf16[8,1408]{1,0:T(8,128)(2,1)S(1)}, u32[]{:S(2)}, u32[]{:S(2)}) %collective-permute-start.1) | collective-permute-done | bytes 22560 | tf_op jit(solution)/shard_map/ppermute | solution.py:292
  8.1 2.7 %collective-permute-start.3 = (bf16[4,8,640]{2,1,0:T(8,128)(2,1)S(1)}, bf16[4,8,640]{2,1,0:T(8,128)(2,1)S(1)}, u32[]{:S(2)}, u32[]{:S(2)}) collective-permute-start(bf16[4,8,640]{2,1,0:T(8,128)(2,1)S(1)} %pad_maximum_fusion.9), channel_id=1, source_target_pairs={{0,4},{1,5},{2,6},{3,7},{4,0},{5,1},{6,2},{7,3},{8,12},{9,13},{10,... | collective-permute-start | bytes 122888 | tf_op jit(solution)/shard_map/ppermute | solution.py:322
  11.1 2.0 %collective-permute-done.3 = bf16[4,8,640]{2,1,0:T(8,128)(2,1)S(1)} collective-permute-done((bf16[4,8,640]{2,1,0:T(8,128)(2,1)S(1)}, bf16[4,8,640]{2,1,0:T(8,128)(2,1)S(1)}, u32[]{:S(2)}, u32[]{:S(2)}) %collective-permute-start.3) | collective-permute-done | bytes 40992 | tf_op jit(solution)/shard_map/ppermute | solution.py:322
  13.1 1.6 %collective-permute-start.4 = (bf16[4,2,8,640]{3,2,0,1:T(8,128)(2,1)S(1)}, bf16[4,2,8,640]{3,2,0,1:T(8,128)(2,1)S(1)}, u32[]{:S(2)}, u32[]{:S(2)}) collective-permute-start(bf16[4,2,8,640]{3,2,0,1:T(8,128)(2,1)S(1)} %pad_maximum_fusion.5), channel_id=1, source_target_pairs={{0,1},{1,0},{2,3},{3,2},{4,5},{5,4},{6,7},{7,6},{8,10},{9,11},{10,... | collective-permute-start | bytes 245768 | tf_op jit(solution)/shard_map/ppermute | solution.py:322
  14.7 1.1 %collective-permute-done.6 = bf16[4,8,768]{2,1,0:T(8,128)(2,1)S(1)} collective-permute-done((bf16[4,8,768]{2,1,0:T(8,128)(2,1)S(1)}, bf16[4,8,768]{2,1,0:T(8,128)(2,1)S(1)}, u32[]{:S(2)}, u32[]{:S(2)}) %collective-permute-start.6) | collective-permute-done | bytes 49184 | tf_op jit(solution)/shard_map/ppermute | solution.py:322
  15.9 1.5 %collective-permute-start.7 = (bf16[4,2,8,768]{3,2,0,1:T(8,128)(2,1)S(1)}, bf16[4,2,8,768]{3,2,0,1:T(8,128)(2,1)S(1)}, u32[]{:S(2)}, u32[]{:S(2)}) collective-permute-start(bf16[4,2,8,768]{3,2,0,1:T(8,128)(2,1)S(1)} %pad_maximum_fusion.4), channel_id=1, source_target_pairs={{0,2},{1,3},{2,0},{3,1},{4,6},{5,7},{6,4},{7,5},{8,9},{9,8},{10,11... | collective-permute-start | bytes 294920 | tf_op jit(solution)/shard_map/ppermute | solution.py:322
  17.4 0.8 %collective-permute-done.4 = bf16[4,2,8,640]{3,2,0,1:T(8,128)(2,1)S(1)} collective-permute-done((bf16[4,2,8,640]{3,2,0,1:T(8,128)(2,1)S(1)}, bf16[4,2,8,640]{3,2,0,1:T(8,128)(2,1)S(1)}, u32[]{:S(2)}, u32[]{:S(2)}) %collective-permute-start.4) | collective-permute-done | bytes 81952 | tf_op jit(solution)/shard_map/ppermute | solution.py:322
  18.3 2.1 %collective-permute-start.5 = (bf16[4,2,2,8,640]{4,3,0,1,2:T(8,128)(2,1)S(1)}, bf16[4,2,2,8,640]{4,3,0,1,2:T(8,128)(2,1)S(1)}, u32[]{:S(2)}, u32[]{:S(2)}) collective-permute-start(bf16[4,2,2,8,640]{4,3,0,1,2:T(8,128)(2,1)S(1)} %pad_maximum_fusion.3), channel_id=1, source_target_pairs={{0,2},{1,3},{2,0},{3,1},{4,6},{5,7},{6,4},{7,5},{8,9},{9,8},{10,11... | collective-permute-start | bytes 491528 | tf_op jit(solution)/shard_map/ppermute | solution.py:322
  20.6 1.6 %collective-permute-start.8 = (bf16[4,2,2,8,768]{4,3,0,1,2:T(8,128)(2,1)S(1)}, bf16[4,2,2,8,768]{4,3,0,1,2:T(8,128)(2,1)S(1)}, u32[]{:S(2)}, u32[]{:S(2)}) collective-permute-start(bf16[4,2,2,8,768]{4,3,0,1,2:T(8,128)(2,1)S(1)} %pad_maximum_fusion.2), channel_id=1, source_target_pairs={{0,1},{1,0},{2,3},{3,2},{4,5},{5,4},{6,7},{7,6},{8,10},{9,11},{10,... | collective-permute-start | bytes 589832 | tf_op jit(solution)/shard_map/ppermute | solution.py:322
  22.2 2.9 %collective-permute-done.5 = bf16[4,2,2,8,640]{4,3,0,1,2:T(8,128)(2,1)S(1)} collective-permute-done((bf16[4,2,2,8,640]{4,3,0,1,2:T(8,128)(2,1)S(1)}, bf16[4,2,2,8,640]{4,3,0,1,2:T(8,128)(2,1)S(1)}, u32[]{:S(2)}, u32[]{:S(2)}) %collective-permute-start.5) | collective-permute-done | bytes 163872 | tf_op jit(solution)/shard_map/ppermute | solution.py:322
  25.1 1.2 %collective-permute-done.8 = bf16[4,2,2,8,768]{4,3,0,1,2:T(8,128)(2,1)S(1)} collective-permute-done((bf16[4,2,2,8,768]{4,3,0,1,2:T(8,128)(2,1)S(1)}, bf16[4,2,2,8,768]{4,3,0,1,2:T(8,128)(2,1)S(1)}, u32[]{:S(2)}, u32[]{:S(2)}) %collective-permute-start.8) | collective-permute-done | bytes 196640 | tf_op jit(solution)/shard_map/ppermute | solution.py:322
  26.5 0.8 %stats.1 = (f32[2,8,256]{2,1,0:T(8,128)S(1)}, f32[5,128,256]{2,1,0:T(8,128)S(1)}, f32[8,256]{1,0:T(8,128)S(1)}, bf16[256,128]{1,0:T(8,128)(2,1)S(1)}) custom-call(s32[8,128]{1,0:T(8,128)S(1)} %get-tuple-element.24.start_ref, bf16[256,768]{1,0:T(8,128)(2,1)S(1)} %bitcast.44, bf16[128,640]{1,0:T(8,128)(2,1)S(1)} %get-tuple-element.22.k_ref), custom_call_target="tpu_custom_call" | custom-call | tf_op jit(solution)/shard_map/stats/pallas_call | solution.py:166
  27.3 1.6 %collective-permute-start.9 = (f32[2,8,256]{2,1,0:T(8,128)S(1)}, f32[2,8,256]{2,1,0:T(8,128)S(1)}, u32[]{:S(2)}, u32[]{:S(2)}) collective-permute-start(f32[2,8,256]{2,1,0:T(8,128)S(1)} %get-tuple-element.30.own_ref), channel_id=1, source_target_pairs={{0,1},{1,0},{2,3},{3,2},{4,5},{5,4},{6,7},{7,6},{8,9},{9,8},{10,11... | collective-permute-start | bytes 49160 | tf_op jit(solution)/shard_map/ppermute | solution.py:292
  28.9 1.4 %query_gradients.1 = (bf16[256,768]{1,0:T(8,128)(2,1)}, bf16[5,128,256]{2,1,0:T(8,128)(2,1)S(1)}) custom-call(bf16[256,640]{1,0:T(8,128)(2,1)S(1)} %bitcast.46, bf16[128,640]{1,0:T(8,128)(2,1)S(1)} %get-tuple-element.22.k_ref, bf16[128,640]{1,0:T(8,128)(2,1)S(1)} %get-tuple-element.23.v_ref, f32[5,128,256]{2,1,0:T(8,128)S(1)} %get-tuple-element.25.p_ref, ...), custom_call_target="tpu_custom_call" | custom-call | tf_op jit(solution)/shard_map/query_gradients/pallas_call | solution.py:205
  30.3 4.5 %all-to-all-start = ((bf16[32,8,768]{2,1,0:T(8,128)(2,1)}), bf16[32,8,768]{2,1,0:T(8,128)(2,1)S(1)}, u32[]{:S(2)}, u32[]{:S(2)}) async-start(bf16[32,8,768]{2,1,0:T(8,128)(2,1)} %bitcast.49), calls=%async_computation | async-start | bytes 786432 | tf_op jit(solution)/shard_map/all_to_all | solution.py:341
  34.9 2.7 %collective-permute-start.10 = (f32[2,8,256]{2,1,0:T(8,128)S(1)}, f32[2,8,256]{2,1,0:T(8,128)S(1)}, u32[]{:S(2)}, u32[]{:S(2)}) collective-permute-start(f32[2,8,256]{2,1,0:T(8,128)S(1)} %pad_maximum_fusion.10), channel_id=1, source_target_pairs={{0,4},{1,5},{2,6},{3,7},{4,0},{5,1},{6,2},{7,3},{8,12},{9,13},{10,... | collective-permute-start | bytes 49160 | tf_op jit(solution)/shard_map/ppermute | solution.py:292
  37.7 10.1 %collective-permute-done.10 = f32[2,8,256]{2,1,0:T(8,128)S(1)} collective-permute-done((f32[2,8,256]{2,1,0:T(8,128)S(1)}, f32[2,8,256]{2,1,0:T(8,128)S(1)}, u32[]{:S(2)}, u32[]{:S(2)}) %collective-permute-start.10) | collective-permute-done | bytes 16416 | tf_op jit(solution)/shard_map/ppermute | solution.py:292
  47.9 3.7 %collective-permute-done.11 = f32[2,8,256]{2,1,0:T(8,128)S(1)} collective-permute-done((f32[2,8,256]{2,1,0:T(8,128)S(1)}, f32[2,8,256]{2,1,0:T(8,128)S(1)}, u32[]{:S(2)}, u32[]{:S(2)}) %collective-permute-start.11) | collective-permute-done | bytes 16416 | tf_op jit(solution)/shard_map/ppermute | solution.py:292
  51.6 1.0 %cache_gradients.1 = (bf16[128,640]{1,0:T(8,128)(2,1)}, bf16[128,640]{1,0:T(8,128)(2,1)}) custom-call(bf16[256,768]{1,0:T(8,128)(2,1)S(1)} %bitcast.45, bf16[256,640]{1,0:T(8,128)(2,1)S(1)} %bitcast.47, f32[5,128,256]{2,1,0:T(8,128)S(1)} %get-tuple-element.25.p_ref, bf16[5,128,256]{2,1,0:T(8,128)(2,1)S(1)} %get-tuple-element.29.ds_ref, ...), custom_call_target="tpu_custom_call" | custom-call | tf_op jit(solution)/shard_map/cache_gradients/pallas_call | solution.py:235
  52.7 1.4 %combine.1 = bf16[8,2560]{1,0:T(8,128)(2,1)} custom-call(bf16[4,8,8,768]{3,2,1,0:T(8,128)(2,1)S(1)} %bitcast.48), custom_call_target="tpu_custom_call" | custom-call | tf_op jit(solution)/shard_map/combine/pallas_call | solution.py:272
  (32 shorter events, 1.1 us)
Async XLA Ops:
  1.8 4.0 %collective-permute-start = (bf16[8,1408]{1,0:T(8,128)(2,1)S(1)}, bf16[8,1408]{1,0:T(8,128)(2,1)S(1)}, u32[]{:S(2)}, u32[]{:S(2)}) collective-permute-start(bf16[8,1408]{1,0:T(8,128)(2,1)S(1)} %get-tuple-element.18), channel_id=1, source_target_pairs={{0,24},{8,16},{16,8},{24,0},{1,25},{9,17},{17,9},{25,1},{2,26},{10... | collective-permute-start | bytes 67592 | tf_op jit(solution)/shard_map/ppermute | solution.py:292
  4.2 3.8 %collective-permute-start.1 = (bf16[8,1408]{1,0:T(8,128)(2,1)S(1)}, bf16[8,1408]{1,0:T(8,128)(2,1)S(1)}, u32[]{:S(2)}, u32[]{:S(2)}) collective-permute-start(bf16[8,1408]{1,0:T(8,128)(2,1)S(1)} %get-tuple-element.19), channel_id=1, source_target_pairs={{0,16},{8,24},{16,0},{24,8},{1,17},{9,25},{17,1},{25,9},{2,18},{10... | collective-permute-start | bytes 67592 | tf_op jit(solution)/shard_map/ppermute | solution.py:292
  4.9 3.2 %collective-permute-start.2 = (bf16[8,1408]{1,0:T(8,128)(2,1)S(1)}, bf16[8,1408]{1,0:T(8,128)(2,1)S(1)}, u32[]{:S(2)}, u32[]{:S(2)}) collective-permute-start(bf16[8,1408]{1,0:T(8,128)(2,1)S(1)} %get-tuple-element.20), channel_id=1, source_target_pairs={{0,8},{8,0},{16,24},{24,16},{1,9},{9,1},{17,25},{25,17},{2,10},{10... | collective-permute-start | bytes 67592 | tf_op jit(solution)/shard_map/ppermute | solution.py:292
  8.1 5.0 %collective-permute-start.3 = (bf16[4,8,640]{2,1,0:T(8,128)(2,1)S(1)}, bf16[4,8,640]{2,1,0:T(8,128)(2,1)S(1)}, u32[]{:S(2)}, u32[]{:S(2)}) collective-permute-start(bf16[4,8,640]{2,1,0:T(8,128)(2,1)S(1)} %pad_maximum_fusion.9), channel_id=1, source_target_pairs={{0,4},{1,5},{2,6},{3,7},{4,0},{5,1},{6,2},{7,3},{8,12},{9,13},{10,... | collective-permute-start | bytes 122888 | tf_op jit(solution)/shard_map/ppermute | solution.py:322
  10.7 5.1 %collective-permute-start.6 = (bf16[4,8,768]{2,1,0:T(8,128)(2,1)S(1)}, bf16[4,8,768]{2,1,0:T(8,128)(2,1)S(1)}, u32[]{:S(2)}, u32[]{:S(2)}) collective-permute-start(bf16[4,8,768]{2,1,0:T(8,128)(2,1)S(1)} %pad_maximum_fusion.6), channel_id=1, source_target_pairs={{0,4},{1,5},{2,6},{3,7},{4,0},{5,1},{6,2},{7,3},{8,12},{9,13},{10,... | collective-permute-start | bytes 147464 | tf_op jit(solution)/shard_map/ppermute | solution.py:322
  13.1 5.1 %collective-permute-start.4 = (bf16[4,2,8,640]{3,2,0,1:T(8,128)(2,1)S(1)}, bf16[4,2,8,640]{3,2,0,1:T(8,128)(2,1)S(1)}, u32[]{:S(2)}, u32[]{:S(2)}) collective-permute-start(bf16[4,2,8,640]{3,2,0,1:T(8,128)(2,1)S(1)} %pad_maximum_fusion.5), channel_id=1, source_target_pairs={{0,1},{1,0},{2,3},{3,2},{4,5},{5,4},{6,7},{7,6},{8,10},{9,11},{10,... | collective-permute-start | bytes 245768 | tf_op jit(solution)/shard_map/ppermute | solution.py:322
  15.9 4.7 %collective-permute-start.7 = (bf16[4,2,8,768]{3,2,0,1:T(8,128)(2,1)S(1)}, bf16[4,2,8,768]{3,2,0,1:T(8,128)(2,1)S(1)}, u32[]{:S(2)}, u32[]{:S(2)}) collective-permute-start(bf16[4,2,8,768]{3,2,0,1:T(8,128)(2,1)S(1)} %pad_maximum_fusion.4), channel_id=1, source_target_pairs={{0,2},{1,3},{2,0},{3,1},{4,6},{5,7},{6,4},{7,5},{8,9},{9,8},{10,11... | collective-permute-start | bytes 294920 | tf_op jit(solution)/shard_map/ppermute | solution.py:322
  18.3 6.8 %collective-permute-start.5 = (bf16[4,2,2,8,640]{4,3,0,1,2:T(8,128)(2,1)S(1)}, bf16[4,2,2,8,640]{4,3,0,1,2:T(8,128)(2,1)S(1)}, u32[]{:S(2)}, u32[]{:S(2)}) collective-permute-start(bf16[4,2,2,8,640]{4,3,0,1,2:T(8,128)(2,1)S(1)} %pad_maximum_fusion.3), channel_id=1, source_target_pairs={{0,2},{1,3},{2,0},{3,1},{4,6},{5,7},{6,4},{7,5},{8,9},{9,8},{10,11... | collective-permute-start | bytes 491528 | tf_op jit(solution)/shard_map/ppermute | solution.py:322
  20.6 5.7 %collective-permute-start.8 = (bf16[4,2,2,8,768]{4,3,0,1,2:T(8,128)(2,1)S(1)}, bf16[4,2,2,8,768]{4,3,0,1,2:T(8,128)(2,1)S(1)}, u32[]{:S(2)}, u32[]{:S(2)}) collective-permute-start(bf16[4,2,2,8,768]{4,3,0,1,2:T(8,128)(2,1)S(1)} %pad_maximum_fusion.2), channel_id=1, source_target_pairs={{0,1},{1,0},{2,3},{3,2},{4,5},{5,4},{6,7},{7,6},{8,10},{9,11},{10,... | collective-permute-start | bytes 589832 | tf_op jit(solution)/shard_map/ppermute | solution.py:322
  27.3 7.6 %collective-permute-start.9 = (f32[2,8,256]{2,1,0:T(8,128)S(1)}, f32[2,8,256]{2,1,0:T(8,128)S(1)}, u32[]{:S(2)}, u32[]{:S(2)}) collective-permute-start(f32[2,8,256]{2,1,0:T(8,128)S(1)} %get-tuple-element.30.own_ref), channel_id=1, source_target_pairs={{0,1},{1,0},{2,3},{3,2},{4,5},{5,4},{6,7},{7,6},{8,9},{9,8},{10,11... | collective-permute-start | bytes 49160 | tf_op jit(solution)/shard_map/ppermute | solution.py:292
  30.3 22.3 %all-to-all-start = ((bf16[32,8,768]{2,1,0:T(8,128)(2,1)}), bf16[32,8,768]{2,1,0:T(8,128)(2,1)S(1)}, u32[]{:S(2)}, u32[]{:S(2)}) async-start(bf16[32,8,768]{2,1,0:T(8,128)(2,1)} %bitcast.49), calls=%async_computation | async-start | bytes 786432 | tf_op jit(solution)/shard_map/all_to_all | solution.py:341
  34.9 12.8 %collective-permute-start.10 = (f32[2,8,256]{2,1,0:T(8,128)S(1)}, f32[2,8,256]{2,1,0:T(8,128)S(1)}, u32[]{:S(2)}, u32[]{:S(2)}) collective-permute-start(f32[2,8,256]{2,1,0:T(8,128)S(1)} %pad_maximum_fusion.10), channel_id=1, source_target_pairs={{0,4},{1,5},{2,6},{3,7},{4,0},{5,1},{6,2},{7,3},{8,12},{9,13},{10,... | collective-permute-start | bytes 49160 | tf_op jit(solution)/shard_map/ppermute | solution.py:292
  47.8 3.8 %collective-permute-start.11 = (f32[2,8,256]{2,1,0:T(8,128)S(1)}, f32[2,8,256]{2,1,0:T(8,128)S(1)}, u32[]{:S(2)}, u32[]{:S(2)}) collective-permute-start(f32[2,8,256]{2,1,0:T(8,128)S(1)} %pad_maximum_fusion.11), channel_id=1, source_target_pairs={{0,2},{1,3},{2,0},{3,1},{4,6},{5,7},{6,4},{7,5},{8,10},{9,11},{10,... | collective-permute-start | bytes 49160 | tf_op jit(solution)/shard_map/ppermute | solution.py:292

commit v2 on v1

--- a/solution.py
+++ b/solution.py
@@ -322,18 +322,19 @@
     return lax.ppermute(value, ("section", "ctx"), pairs)
 
 
-def spread_blocks(blocks, first_bits, last_bits):
+def spread_blocks(blocks, even_bits, odd_bits):
     count = lax.axis_size("ctx")
     at = lax.axis_index("ctx")
     odd = lax.axis_index("section") % 2 == 1
     lead, rest = blocks.shape[0], blocks.shape[1:]
-    pairs = [(bit, bit) for bit in first_bits] + [last_bits, last_bits[::-1]]
-    for i, (even_bit, odd_bit) in enumerate(pairs):
+    for i, (even_bit, odd_bit) in enumerate(zip(even_bits, odd_bits)):
         upper = at >> jnp.where(odd, odd_bit, even_bit) & 1 == 1
         other = flip_by_parity(blocks, (even_bit, odd_bit))
         blocks = ordered(blocks, other, upper, 1 + i)
-    turned = odd if last_bits[0] > last_bits[1] else ~odd
-    blocks = jnp.where(turned, jnp.swapaxes(blocks, i, i + 1), blocks)
+    turned = [bits[-2] < bits[-1] for bits in (even_bits, odd_bits)]
+    if any(turned):
+        other = jnp.swapaxes(blocks, i, i + 1)
+        blocks = jnp.where(jnp.where(odd, turned[1], turned[0]), other, blocks)
     return blocks.reshape((lead, count) + rest)
 
 
@@ -368,10 +369,10 @@
     start, keys, values = packed[sections:]
     swapped = swap_blocks(packed[:sections], "section")
     query_all, grad_all = swapped[..., : here + LANES], swapped[..., here + LANES :]
-    last = (down[-2], down[-1])
-    query_all = spread_blocks(query_all, down[:-2], last)
+    turned = down[:-2] + [down[-1], down[-2]]
+    query_all = spread_blocks(query_all, down, down)
     query_all = query_all.reshape(peers * rows, here + LANES)
-    grad_all = spread_blocks(grad_all, down[:-2], last[::-1])
+    grad_all = spread_blocks(grad_all, turned, down)
     grad_all = grad_all.reshape(peers * rows, here)
 
     own, probs, deltas, row_stats = stats_kernel(start, query_all, keys, row_count, key_total)

time: 54.3 us -> 53.9 us (level)
  no operation moved by 1% of the time
where the time goes in v2:
time: 53.9 us; the launch traced here: 53.7 us
  waiting for transfers between devices  25.1 us (47%)
  starting transfers between devices  21.6 us (40%)
  Pallas kernels  5.72 us (11%)
  between operations  0.82 us (2%)
    ppermute x6, waiting for transfers between devices, flip(): return lax.ppermute(value, axis, [(i, i ^ bit) for i in range(count)])  16.9 us
    ppermute x6, starting transfers between devices, flip_by_parity(): return lax.ppermute(value, ('section', 'ctx'), pairs)  9.83 us
    ppermute x6, waiting for transfers between devices, flip_by_parity(): return lax.ppermute(value, ('section', 'ctx'), pairs)  8.14 us
    ppermute x6, starting transfers between devices, flip(): return lax.ppermute(value, axis, [(i, i ^ bit) for i in range(count)])  7.54 us
    all_to_all x1, starting transfers between devices, exchange(): return lax.all_to_all(blocks, ('section', 'ctx'), 0, 0, tiled=True)  4.23 us
    pallas_call x1, Pallas kernels, query_kernel(): pl.pallas_call(body, in_specs=in_vmem(6), out_specs=[pl.BlockSpec(memory_...  1.41 us
    pallas_call x1, Pallas kernels, combine_kernel(): pl.pallas_call(body, in_specs=in_vmem(1), out_specs=in_vmem(1)[0], out_sh...  1.37 us
    pallas_call x1, Pallas kernels, pack(): pl.pallas_call(body, in_specs=[pl.BlockSpec(memory_space=pl.ANY)] * 6, ou...  1.12 us
  transfers between devices with their start and end apart: 13, of which 10 were waited for; matrix products, arithmetic and copies ran while one was open for 1% of the time, Pallas kernels for 5%

profile of v2, /device:TPU:0, one launch (start us, length us, event | category | flops | bytes accessed | tf_op | source)
XLA Modules:
  0.0 53.7 jit_solution(15359712701258598962)
XLA Ops:
  0.6 1.1 %pack.1 = (bf16[8,1408]{1,0:T(8,128)(2,1)S(1)}, bf16[8,1408]{1,0:T(8,128)(2,1)S(1)}, bf16[8,1408]{1,0:T(8,128)(2,1)S(1)}, bf16[8,1408]{1,0:T(8,128)(2,1)S(1)}, s...) custom-call(s32[8]{0:T(128)} %order_hbm.1, bf16[128,640]{1,0:T(8,128)(2,1)} %k_hbm.1, ...), custom_call_target="tpu_custom_call" | custom-call | tf_op jit(solution)/shard_map/pack/pallas_call | solution.py:109
  1.8 2.5 %collective-permute-start = (bf16[8,1408]{1,0:T(8,128)(2,1)S(1)}, bf16[8,1408]{1,0:T(8,128)(2,1)S(1)}, u32[]{:S(2)}, u32[]{:S(2)}) collective-permute-start(bf16[8,1408]{1,0:T(8,128)(2,1)S(1)} %get-tuple-element.18), channel_id=1, source_target_pairs={{0,24},{8,16},{16,8},{24,0},{1,25},{9,17},{17,9},{25,1},{2,26},{10... | collective-permute-start | bytes 67592 | tf_op jit(solution)/shard_map/ppermute | solution.py:292
  4.2 0.6 %collective-permute-start.1 = (bf16[8,1408]{1,0:T(8,128)(2,1)S(1)}, bf16[8,1408]{1,0:T(8,128)(2,1)S(1)}, u32[]{:S(2)}, u32[]{:S(2)}) collective-permute-start(bf16[8,1408]{1,0:T(8,128)(2,1)S(1)} %get-tuple-element.19), channel_id=1, source_target_pairs={{0,16},{8,24},{16,0},{24,8},{1,17},{9,25},{17,1},{25,9},{2,18},{10... | collective-permute-start | bytes 67592 | tf_op jit(solution)/shard_map/ppermute | solution.py:292
  4.9 0.9 %collective-permute-done = bf16[8,1408]{1,0:T(8,128)(2,1)S(1)} collective-permute-done((bf16[8,1408]{1,0:T(8,128)(2,1)S(1)}, bf16[8,1408]{1,0:T(8,128)(2,1)S(1)}, u32[]{:S(2)}, u32[]{:S(2)}) %collective-permute-start) | collective-permute-done | bytes 22560 | tf_op jit(solution)/shard_map/ppermute | solution.py:292
  5.8 2.2 %collective-permute-done.1 = bf16[8,1408]{1,0:T(8,128)(2,1)S(1)} collective-permute-done((bf16[8,1408]{1,0:T(8,128)(2,1)S(1)}, bf16[8,1408]{1,0:T(8,128)(2,1)S(1)}, u32[]{:S(2)}, u32[]{:S(2)}) %collective-permute-start.1) | collective-permute-done | bytes 22560 | tf_op jit(solution)/shard_map/ppermute | solution.py:292
  8.1 2.7 %collective-permute-start.3 = (bf16[4,8,640]{2,1,0:T(8,128)(2,1)S(1)}, bf16[4,8,640]{2,1,0:T(8,128)(2,1)S(1)}, u32[]{:S(2)}, u32[]{:S(2)}) collective-permute-start(bf16[4,8,640]{2,1,0:T(8,128)(2,1)S(1)} %pad_maximum_fusion.9), channel_id=1, source_target_pairs={{0,4},{1,5},{2,6},{3,7},{4,0},{5,1},{6,2},{7,3},{8,12},{9,13},{10,... | collective-permute-start | bytes 122888 | tf_op jit(solution)/shard_map/ppermute | solution.py:322
  11.1 2.0 %collective-permute-done.3 = bf16[4,8,640]{2,1,0:T(8,128)(2,1)S(1)} collective-permute-done((bf16[4,8,640]{2,1,0:T(8,128)(2,1)S(1)}, bf16[4,8,640]{2,1,0:T(8,128)(2,1)S(1)}, u32[]{:S(2)}, u32[]{:S(2)}) %collective-permute-start.3) | collective-permute-done | bytes 40992 | tf_op jit(solution)/shard_map/ppermute | solution.py:322
  13.1 1.6 %collective-permute-start.4 = (bf16[4,2,8,640]{3,2,0,1:T(8,128)(2,1)S(1)}, bf16[4,2,8,640]{3,2,0,1:T(8,128)(2,1)S(1)}, u32[]{:S(2)}, u32[]{:S(2)}) collective-permute-start(bf16[4,2,8,640]{3,2,0,1:T(8,128)(2,1)S(1)} %pad_maximum_fusion.5), channel_id=1, source_target_pairs={{0,1},{1,0},{2,3},{3,2},{4,5},{5,4},{6,7},{7,6},{8,10},{9,11},{10,... | collective-permute-start | bytes 245768 | tf_op jit(solution)/shard_map/ppermute | solution.py:322
  14.7 1.1 %collective-permute-done.6 = bf16[4,8,768]{2,1,0:T(8,128)(2,1)S(1)} collective-permute-done((bf16[4,8,768]{2,1,0:T(8,128)(2,1)S(1)}, bf16[4,8,768]{2,1,0:T(8,128)(2,1)S(1)}, u32[]{:S(2)}, u32[]{:S(2)}) %collective-permute-start.6) | collective-permute-done | bytes 49184 | tf_op jit(solution)/shard_map/ppermute | solution.py:322
  15.9 1.5 %collective-permute-start.7 = (bf16[4,2,8,768]{3,2,0,1:T(8,128)(2,1)S(1)}, bf16[4,2,8,768]{3,2,0,1:T(8,128)(2,1)S(1)}, u32[]{:S(2)}, u32[]{:S(2)}) collective-permute-start(bf16[4,2,8,768]{3,2,0,1:T(8,128)(2,1)S(1)} %pad_maximum_fusion.4), channel_id=1, source_target_pairs={{0,2},{1,3},{2,0},{3,1},{4,6},{5,7},{6,4},{7,5},{8,10},{9,11},{10,... | collective-permute-start | bytes 294920 | tf_op jit(solution)/shard_map/ppermute | solution.py:322
  17.7 2.1 %collective-permute-start.5 = (bf16[4,2,2,8,640]{4,3,0,1,2:T(8,128)(2,1)S(1)}, bf16[4,2,2,8,640]{4,3,0,1,2:T(8,128)(2,1)S(1)}, u32[]{:S(2)}, u32[]{:S(2)}) collective-permute-start(bf16[4,2,2,8,640]{4,3,0,1,2:T(8,128)(2,1)S(1)} %pad_maximum_fusion.3), channel_id=1, source_target_pairs={{0,2},{1,3},{2,0},{3,1},{4,6},{5,7},{6,4},{7,5},{8,9},{9,8},{10,11... | collective-permute-start | bytes 491528 | tf_op jit(solution)/shard_map/ppermute | solution.py:322
  19.8 0.8 %collective-permute-done.7 = bf16[4,2,8,768]{3,2,0,1:T(8,128)(2,1)S(1)} collective-permute-done((bf16[4,2,8,768]{3,2,0,1:T(8,128)(2,1)S(1)}, bf16[4,2,8,768]{3,2,0,1:T(8,128)(2,1)S(1)}, u32[]{:S(2)}, u32[]{:S(2)}) %collective-permute-start.7) | collective-permute-done | bytes 98336 | tf_op jit(solution)/shard_map/ppermute | solution.py:322
  20.6 1.6 %collective-permute-start.8 = (bf16[4,2,2,8,768]{4,3,0,1,2:T(8,128)(2,1)S(1)}, bf16[4,2,2,8,768]{4,3,0,1,2:T(8,128)(2,1)S(1)}, u32[]{:S(2)}, u32[]{:S(2)}) collective-permute-start(bf16[4,2,2,8,768]{4,3,0,1,2:T(8,128)(2,1)S(1)} %pad_maximum_fusion.2), channel_id=1, source_target_pairs={{0,1},{1,0},{2,3},{3,2},{4,5},{5,4},{6,7},{7,6},{8,9},{9,8},{10,11... | collective-permute-start | bytes 589832 | tf_op jit(solution)/shard_map/ppermute | solution.py:322
  22.2 0.9 %collective-permute-done.5 = bf16[4,2,2,8,640]{4,3,0,1,2:T(8,128)(2,1)S(1)} collective-permute-done((bf16[4,2,2,8,640]{4,3,0,1,2:T(8,128)(2,1)S(1)}, bf16[4,2,2,8,640]{4,3,0,1,2:T(8,128)(2,1)S(1)}, u32[]{:S(2)}, u32[]{:S(2)}) %collective-permute-start.5) | collective-permute-done | bytes 163872 | tf_op jit(solution)/shard_map/ppermute | solution.py:322
  23.2 3.2 %collective-permute-done.8 = bf16[4,2,2,8,768]{4,3,0,1,2:T(8,128)(2,1)S(1)} collective-permute-done((bf16[4,2,2,8,768]{4,3,0,1,2:T(8,128)(2,1)S(1)}, bf16[4,2,2,8,768]{4,3,0,1,2:T(8,128)(2,1)S(1)}, u32[]{:S(2)}, u32[]{:S(2)}) %collective-permute-start.8) | collective-permute-done | bytes 196640 | tf_op jit(solution)/shard_map/ppermute | solution.py:322
  26.5 0.8 %stats.1 = (f32[2,8,256]{2,1,0:T(8,128)S(1)}, f32[5,128,256]{2,1,0:T(8,128)S(1)}, f32[8,256]{1,0:T(8,128)S(1)}, bf16[256,128]{1,0:T(8,128)(2,1)S(1)}) custom-call(s32[8,128]{1,0:T(8,128)S(1)} %get-tuple-element.24.start_ref, bf16[256,768]{1,0:T(8,128)(2,1)S(1)} %bitcast.42, bf16[128,640]{1,0:T(8,128)(2,1)S(1)} %get-tuple-element.22.k_ref), custom_call_target="tpu_custom_call" | custom-call | tf_op jit(solution)/shard_map/stats/pallas_call | solution.py:166
  27.2 1.6 %collective-permute-start.9 = (f32[2,8,256]{2,1,0:T(8,128)S(1)}, f32[2,8,256]{2,1,0:T(8,128)S(1)}, u32[]{:S(2)}, u32[]{:S(2)}) collective-permute-start(f32[2,8,256]{2,1,0:T(8,128)S(1)} %get-tuple-element.30.own_ref), channel_id=1, source_target_pairs={{0,1},{1,0},{2,3},{3,2},{4,5},{5,4},{6,7},{7,6},{8,9},{9,8},{10,11... | collective-permute-start | bytes 49160 | tf_op jit(solution)/shard_map/ppermute | solution.py:292
  28.9 1.4 %query_gradients.1 = (bf16[256,768]{1,0:T(8,128)(2,1)}, bf16[5,128,256]{2,1,0:T(8,128)(2,1)S(1)}) custom-call(bf16[256,640]{1,0:T(8,128)(2,1)S(1)} %bitcast.44, bf16[128,640]{1,0:T(8,128)(2,1)S(1)} %get-tuple-element.22.k_ref, bf16[128,640]{1,0:T(8,128)(2,1)S(1)} %get-tuple-element.23.v_ref, f32[5,128,256]{2,1,0:T(8,128)S(1)} %get-tuple-element.25.p_ref, ...), custom_call_target="tpu_custom_call" | custom-call | tf_op jit(solution)/shard_map/query_gradients/pallas_call | solution.py:205
  30.3 4.2 %all-to-all-start = ((bf16[32,8,768]{2,1,0:T(8,128)(2,1)}), bf16[32,8,768]{2,1,0:T(8,128)(2,1)S(1)}, u32[]{:S(2)}, u32[]{:S(2)}) async-start(bf16[32,8,768]{2,1,0:T(8,128)(2,1)} %bitcast.47), calls=%async_computation | async-start | bytes 786432 | tf_op jit(solution)/shard_map/all_to_all | solution.py:342
  34.6 2.7 %collective-permute-start.10 = (f32[2,8,256]{2,1,0:T(8,128)S(1)}, f32[2,8,256]{2,1,0:T(8,128)S(1)}, u32[]{:S(2)}, u32[]{:S(2)}) collective-permute-start(f32[2,8,256]{2,1,0:T(8,128)S(1)} %pad_maximum_fusion.10), channel_id=1, source_target_pairs={{0,4},{1,5},{2,6},{3,7},{4,0},{5,1},{6,2},{7,3},{8,12},{9,13},{10,... | collective-permute-start | bytes 49160 | tf_op jit(solution)/shard_map/ppermute | solution.py:292
  37.3 10.1 %collective-permute-done.10 = f32[2,8,256]{2,1,0:T(8,128)S(1)} collective-permute-done((f32[2,8,256]{2,1,0:T(8,128)S(1)}, f32[2,8,256]{2,1,0:T(8,128)S(1)}, u32[]{:S(2)}, u32[]{:S(2)}) %collective-permute-start.10) | collective-permute-done | bytes 16416 | tf_op jit(solution)/shard_map/ppermute | solution.py:292
  47.5 3.7 %collective-permute-done.11 = f32[2,8,256]{2,1,0:T(8,128)S(1)} collective-permute-done((f32[2,8,256]{2,1,0:T(8,128)S(1)}, f32[2,8,256]{2,1,0:T(8,128)S(1)}, u32[]{:S(2)}, u32[]{:S(2)}) %collective-permute-start.11) | collective-permute-done | bytes 16416 | tf_op jit(solution)/shard_map/ppermute | solution.py:292
  51.3 1.0 %cache_gradients.1 = (bf16[128,640]{1,0:T(8,128)(2,1)}, bf16[128,640]{1,0:T(8,128)(2,1)}) custom-call(bf16[256,768]{1,0:T(8,128)(2,1)S(1)} %bitcast.43, bf16[256,640]{1,0:T(8,128)(2,1)S(1)} %bitcast.45, f32[5,128,256]{2,1,0:T(8,128)S(1)} %get-tuple-element.25.p_ref, bf16[5,128,256]{2,1,0:T(8,128)(2,1)S(1)} %get-tuple-element.29.ds_ref, ...), custom_call_target="tpu_custom_call" | custom-call | tf_op jit(solution)/shard_map/cache_gradients/pallas_call | solution.py:235
  52.3 1.4 %combine.1 = bf16[8,2560]{1,0:T(8,128)(2,1)} custom-call(bf16[4,8,8,768]{3,2,1,0:T(8,128)(2,1)S(1)} %bitcast.46), custom_call_target="tpu_custom_call" | custom-call | tf_op jit(solution)/shard_map/combine/pallas_call | solution.py:272
  (31 shorter events, 1.1 us)
Async XLA Ops:
  1.8 4.0 %collective-permute-start = (bf16[8,1408]{1,0:T(8,128)(2,1)S(1)}, bf16[8,1408]{1,0:T(8,128)(2,1)S(1)}, u32[]{:S(2)}, u32[]{:S(2)}) collective-permute-start(bf16[8,1408]{1,0:T(8,128)(2,1)S(1)} %get-tuple-element.18), channel_id=1, source_target_pairs={{0,24},{8,16},{16,8},{24,0},{1,25},{9,17},{17,9},{25,1},{2,26},{10... | collective-permute-start | bytes 67592 | tf_op jit(solution)/shard_map/ppermute | solution.py:292
  4.2 3.8 %collective-permute-start.1 = (bf16[8,1408]{1,0:T(8,128)(2,1)S(1)}, bf16[8,1408]{1,0:T(8,128)(2,1)S(1)}, u32[]{:S(2)}, u32[]{:S(2)}) collective-permute-start(bf16[8,1408]{1,0:T(8,128)(2,1)S(1)} %get-tuple-element.19), channel_id=1, source_target_pairs={{0,16},{8,24},{16,0},{24,8},{1,17},{9,25},{17,1},{25,9},{2,18},{10... | collective-permute-start | bytes 67592 | tf_op jit(solution)/shard_map/ppermute | solution.py:292
  4.9 3.2 %collective-permute-start.2 = (bf16[8,1408]{1,0:T(8,128)(2,1)S(1)}, bf16[8,1408]{1,0:T(8,128)(2,1)S(1)}, u32[]{:S(2)}, u32[]{:S(2)}) collective-permute-start(bf16[8,1408]{1,0:T(8,128)(2,1)S(1)} %get-tuple-element.20), channel_id=1, source_target_pairs={{0,8},{8,0},{16,24},{24,16},{1,9},{9,1},{17,25},{25,17},{2,10},{10... | collective-permute-start | bytes 67592 | tf_op jit(solution)/shard_map/ppermute | solution.py:292
  8.1 5.0 %collective-permute-start.3 = (bf16[4,8,640]{2,1,0:T(8,128)(2,1)S(1)}, bf16[4,8,640]{2,1,0:T(8,128)(2,1)S(1)}, u32[]{:S(2)}, u32[]{:S(2)}) collective-permute-start(bf16[4,8,640]{2,1,0:T(8,128)(2,1)S(1)} %pad_maximum_fusion.9), channel_id=1, source_target_pairs={{0,4},{1,5},{2,6},{3,7},{4,0},{5,1},{6,2},{7,3},{8,12},{9,13},{10,... | collective-permute-start | bytes 122888 | tf_op jit(solution)/shard_map/ppermute | solution.py:322
  10.7 5.1 %collective-permute-start.6 = (bf16[4,8,768]{2,1,0:T(8,128)(2,1)S(1)}, bf16[4,8,768]{2,1,0:T(8,128)(2,1)S(1)}, u32[]{:S(2)}, u32[]{:S(2)}) collective-permute-start(bf16[4,8,768]{2,1,0:T(8,128)(2,1)S(1)} %pad_maximum_fusion.6), channel_id=1, source_target_pairs={{0,4},{1,5},{2,6},{3,7},{4,0},{5,1},{6,2},{7,3},{8,12},{9,13},{10,... | collective-permute-start | bytes 147464 | tf_op jit(solution)/shard_map/ppermute | solution.py:322
  13.1 4.5 %collective-permute-start.4 = (bf16[4,2,8,640]{3,2,0,1:T(8,128)(2,1)S(1)}, bf16[4,2,8,640]{3,2,0,1:T(8,128)(2,1)S(1)}, u32[]{:S(2)}, u32[]{:S(2)}) collective-permute-start(bf16[4,2,8,640]{3,2,0,1:T(8,128)(2,1)S(1)} %pad_maximum_fusion.5), channel_id=1, source_target_pairs={{0,1},{1,0},{2,3},{3,2},{4,5},{5,4},{6,7},{7,6},{8,10},{9,11},{10,... | collective-permute-start | bytes 245768 | tf_op jit(solution)/shard_map/ppermute | solution.py:322
  15.9 4.7 %collective-permute-start.7 = (bf16[4,2,8,768]{3,2,0,1:T(8,128)(2,1)S(1)}, bf16[4,2,8,768]{3,2,0,1:T(8,128)(2,1)S(1)}, u32[]{:S(2)}, u32[]{:S(2)}) collective-permute-start(bf16[4,2,8,768]{3,2,0,1:T(8,128)(2,1)S(1)} %pad_maximum_fusion.4), channel_id=1, source_target_pairs={{0,2},{1,3},{2,0},{3,1},{4,6},{5,7},{6,4},{7,5},{8,10},{9,11},{10,... | collective-permute-start | bytes 294920 | tf_op jit(solution)/shard_map/ppermute | solution.py:322
  17.7 5.4 %collective-permute-start.5 = (bf16[4,2,2,8,640]{4,3,0,1,2:T(8,128)(2,1)S(1)}, bf16[4,2,2,8,640]{4,3,0,1,2:T(8,128)(2,1)S(1)}, u32[]{:S(2)}, u32[]{:S(2)}) collective-permute-start(bf16[4,2,2,8,640]{4,3,0,1,2:T(8,128)(2,1)S(1)} %pad_maximum_fusion.3), channel_id=1, source_target_pairs={{0,2},{1,3},{2,0},{3,1},{4,6},{5,7},{6,4},{7,5},{8,9},{9,8},{10,11... | collective-permute-start | bytes 491528 | tf_op jit(solution)/shard_map/ppermute | solution.py:322
  20.6 5.7 %collective-permute-start.8 = (bf16[4,2,2,8,768]{4,3,0,1,2:T(8,128)(2,1)S(1)}, bf16[4,2,2,8,768]{4,3,0,1,2:T(8,128)(2,1)S(1)}, u32[]{:S(2)}, u32[]{:S(2)}) collective-permute-start(bf16[4,2,2,8,768]{4,3,0,1,2:T(8,128)(2,1)S(1)} %pad_maximum_fusion.2), channel_id=1, source_target_pairs={{0,1},{1,0},{2,3},{3,2},{4,5},{5,4},{6,7},{7,6},{8,9},{9,8},{10,11... | collective-permute-start | bytes 589832 | tf_op jit(solution)/shard_map/ppermute | solution.py:322
  27.2 7.3 %collective-permute-start.9 = (f32[2,8,256]{2,1,0:T(8,128)S(1)}, f32[2,8,256]{2,1,0:T(8,128)S(1)}, u32[]{:S(2)}, u32[]{:S(2)}) collective-permute-start(f32[2,8,256]{2,1,0:T(8,128)S(1)} %get-tuple-element.30.own_ref), channel_id=1, source_target_pairs={{0,1},{1,0},{2,3},{3,2},{4,5},{5,4},{6,7},{7,6},{8,9},{9,8},{10,11... | collective-permute-start | bytes 49160 | tf_op jit(solution)/shard_map/ppermute | solution.py:292
  30.3 22.0 %all-to-all-start = ((bf16[32,8,768]{2,1,0:T(8,128)(2,1)}), bf16[32,8,768]{2,1,0:T(8,128)(2,1)S(1)}, u32[]{:S(2)}, u32[]{:S(2)}) async-start(bf16[32,8,768]{2,1,0:T(8,128)(2,1)} %bitcast.47), calls=%async_computation | async-start | bytes 786432 | tf_op jit(solution)/shard_map/all_to_all | solution.py:342
  34.6 12.8 %collective-permute-start.10 = (f32[2,8,256]{2,1,0:T(8,128)S(1)}, f32[2,8,256]{2,1,0:T(8,128)S(1)}, u32[]{:S(2)}, u32[]{:S(2)}) collective-permute-start(f32[2,8,256]{2,1,0:T(8,128)S(1)} %pad_maximum_fusion.10), channel_id=1, source_target_pairs={{0,4},{1,5},{2,6},{3,7},{4,0},{5,1},{6,2},{7,3},{8,12},{9,13},{10,... | collective-permute-start | bytes 49160 | tf_op jit(solution)/shard_map/ppermute | solution.py:292
  47.4 3.8 %collective-permute-start.11 = (f32[2,8,256]{2,1,0:T(8,128)S(1)}, f32[2,8,256]{2,1,0:T(8,128)S(1)}, u32[]{:S(2)}, u32[]{:S(2)}) collective-permute-start(f32[2,8,256]{2,1,0:T(8,128)S(1)} %pad_maximum_fusion.11), channel_id=1, source_target_pairs={{0,2},{1,3},{2,0},{3,1},{4,6},{5,7},{6,4},{7,5},{8,10},{9,11},{10,... | collective-permute-start | bytes 49160 | tf_op jit(solution)/shard_map/ppermute | solution.py:292

commit v3 on v0

--- a/solution.py
+++ b/solution.py
@@ -241,33 +241,28 @@
     )(vmem(queries), vmem(grads), vmem(probs), vmem(score_grads), vmem(own), vmem(merged))
 
 
-def combine_kernel(parts):
-    sections, holders, rows, width = parts.shape
+def combine_kernel(parts, sections, holders):
+    width = parts.shape[1]
+    rows = parts.shape[0] // (sections * holders)
     here = width - LANES
     heads = here // HEAD_DIM
+    shape = (sections, holders, rows, HEAD_DIM)
 
     def body(p_ref, out_ref):
-        def stats_of(s, c):
-            e = p_ref[s, c, :, pl.ds(here, LANES)].astype(F32)
-            e += pltpu.roll(e, LANES - heads, 1) + pltpu.roll(e, LANES - 2 * heads, 1)
-            return e, pltpu.roll(e, LANES - 3 * heads, 1)
-
-        for s in range(sections):
-            top = jnp.full((rows, LANES), -jnp.inf, F32)
-            for c in range(holders):
-                top = jnp.maximum(top, stats_of(s, c)[0])
-            total = jnp.zeros((rows, LANES), F32)
-            for c in range(holders):
-                own, count = stats_of(s, c)
-                total += jnp.exp(own - top) * count
-            sums = [jnp.zeros((rows, HEAD_DIM), F32) for _ in range(heads)]
-            for c in range(holders):
-                share = jnp.exp(stats_of(s, c)[0] - top) / total
-                for h in range(heads):
-                    value = p_ref[s, c, :, head_of(h)].astype(F32)
-                    sums[h] += share[:, h : h + 1] * value
-            for h in range(heads):
-                out_ref[:, head_of(s * heads + h)] = sums[h].astype(BF)
+        stats = p_ref[:, pl.ds(here, LANES)]
+        lane = lax.broadcasted_iota(jnp.int32, (LANES, HEAD_DIM), 0)
+        for h in range(heads):
+            mine = lane % heads == h
+            first = mine & (lane < 3 * heads)
+            second = mine & (lane >= 3 * heads) & (lane < 6 * heads)
+            own = nn(stats, jnp.where(first, 1.0, 0.0).astype(BF)).reshape(shape)
+            count = nn(stats, jnp.where(second, 1.0, 0.0).astype(BF)).reshape(shape)
+            share = jnp.exp(own - jnp.max(own, axis=1, keepdims=True))
+            total = jnp.sum(share * count, axis=1)
+            value = p_ref[:, head_of(h)].astype(F32).reshape(shape)
+            result = jnp.sum(share * value, axis=1) / total
+            for s in range(sections):
+                out_ref[:, head_of(s * heads + h)] = result[s].astype(BF)
 
     return pl.pallas_call(
         body,
@@ -365,7 +360,8 @@
     part, score_grads = query_kernel(grad_all, keys, values, probs, deltas, row_stats)
     part = exchange(part.reshape(peers, rows, here + LANES))
     grad_keys, grad_values = cache_kernel(query_all, grad_all, probs, score_grads, own, merged)
-    grad_queries = combine_kernel(part.reshape(sections, ctx_count, rows, here + LANES))
+    part = part.reshape(peers * rows, here + LANES)
+    grad_queries = combine_kernel(part, sections, ctx_count)
     return (grad_queries[None], grad_keys, grad_values)
 
 

time: 54.4 us -> 54 us (level)
  no operation moved by 1% of the time
where the time goes in v3:
time: 54 us; the launch traced here: 53.7 us
  waiting for transfers between devices  25.5 us (47%)
  starting transfers between devices  21.7 us (40%)
  Pallas kernels  5.32 us (10%)
  between operations  0.82 us (2%)
    ppermute x12, waiting for transfers between devices, flip(): return lax.ppermute(value, axis, [(i, i ^ bit) for i in range(count)])  25.5 us
    ppermute x12, starting transfers between devices, flip(): return lax.ppermute(value, axis, [(i, i ^ bit) for i in range(count)])  17.5 us
    all_to_all x1, starting transfers between devices, exchange(): return lax.all_to_all(blocks, ('section', 'ctx'), 0, 0, tiled=True)  4.19 us
    pallas_call x1, Pallas kernels, query_kernel(): pl.pallas_call(body, in_specs=in_vmem(6), out_specs=[pl.BlockSpec(memory_...  1.41 us
    pallas_call x1, Pallas kernels, pack(): pl.pallas_call(body, in_specs=[pl.BlockSpec(memory_space=pl.ANY)] * 6, ou...  1.12 us
  transfers between devices with their start and end apart: 13, of which 10 were waited for; matrix products, arithmetic and copies ran while one was open for 1% of the time, Pallas kernels for 5%

profile of v3, /device:TPU:0, one launch (start us, length us, event | category | flops | bytes accessed | tf_op | source)
XLA Modules:
  0.0 53.7 jit_solution(17727410191451323071)
XLA Ops:
  0.6 1.1 %pack.1 = (bf16[8,1408]{1,0:T(8,128)(2,1)S(1)}, bf16[8,1408]{1,0:T(8,128)(2,1)S(1)}, bf16[8,1408]{1,0:T(8,128)(2,1)S(1)}, bf16[8,1408]{1,0:T(8,128)(2,1)S(1)}, s...) custom-call(s32[8]{0:T(128)} %order_hbm.1, bf16[128,640]{1,0:T(8,128)(2,1)} %k_hbm.1, ...), custom_call_target="tpu_custom_call" | custom-call | tf_op jit(solution)/shard_map/pack/pallas_call | solution.py:109
  1.8 2.5 %collective-permute-start = (bf16[8,1408]{1,0:T(8,128)(2,1)S(1)}, bf16[8,1408]{1,0:T(8,128)(2,1)S(1)}, u32[]{:S(2)}, u32[]{:S(2)}) collective-permute-start(bf16[8,1408]{1,0:T(8,128)(2,1)S(1)} %get-tuple-element.18), channel_id=1, source_target_pairs={{0,24},{8,16},{16,8},{24,0},{1,25},{9,17},{17,9},{25,1},{2,26},{10... | collective-permute-start | bytes 67592 | tf_op jit(solution)/shard_map/ppermute | solution.py:287
  4.2 0.6 %collective-permute-start.1 = (bf16[8,1408]{1,0:T(8,128)(2,1)S(1)}, bf16[8,1408]{1,0:T(8,128)(2,1)S(1)}, u32[]{:S(2)}, u32[]{:S(2)}) collective-permute-start(bf16[8,1408]{1,0:T(8,128)(2,1)S(1)} %get-tuple-element.19), channel_id=1, source_target_pairs={{0,16},{8,24},{16,0},{24,8},{1,17},{9,25},{17,1},{25,9},{2,18},{10... | collective-permute-start | bytes 67592 | tf_op jit(solution)/shard_map/ppermute | solution.py:287
  4.9 0.9 %collective-permute-done = bf16[8,1408]{1,0:T(8,128)(2,1)S(1)} collective-permute-done((bf16[8,1408]{1,0:T(8,128)(2,1)S(1)}, bf16[8,1408]{1,0:T(8,128)(2,1)S(1)}, u32[]{:S(2)}, u32[]{:S(2)}) %collective-permute-start) | collective-permute-done | bytes 22560 | tf_op jit(solution)/shard_map/ppermute | solution.py:287
  5.8 2.2 %collective-permute-done.1 = bf16[8,1408]{1,0:T(8,128)(2,1)S(1)} collective-permute-done((bf16[8,1408]{1,0:T(8,128)(2,1)S(1)}, bf16[8,1408]{1,0:T(8,128)(2,1)S(1)}, u32[]{:S(2)}, u32[]{:S(2)}) %collective-permute-start.1) | collective-permute-done | bytes 22560 | tf_op jit(solution)/shard_map/ppermute | solution.py:287
  8.1 2.7 %collective-permute-start.3 = (bf16[4,8,640]{2,1,0:T(8,128)(2,1)S(1)}, bf16[4,8,640]{2,1,0:T(8,128)(2,1)S(1)}, u32[]{:S(2)}, u32[]{:S(2)}) collective-permute-start(bf16[4,8,640]{2,1,0:T(8,128)(2,1)S(1)} %pad_maximum_fusion.9), channel_id=1, source_target_pairs={{0,4},{1,5},{2,6},{3,7},{4,0},{5,1},{6,2},{7,3},{8,12},{9,13},{10,... | collective-permute-start | bytes 122888 | tf_op jit(solution)/shard_map/ppermute | solution.py:287
  11.1 2.0 %collective-permute-done.3 = bf16[4,8,640]{2,1,0:T(8,128)(2,1)S(1)} collective-permute-done((bf16[4,8,640]{2,1,0:T(8,128)(2,1)S(1)}, bf16[4,8,640]{2,1,0:T(8,128)(2,1)S(1)}, u32[]{:S(2)}, u32[]{:S(2)}) %collective-permute-start.3) | collective-permute-done | bytes 40992 | tf_op jit(solution)/shard_map/ppermute | solution.py:287
  13.1 1.6 %collective-permute-start.4 = (bf16[4,2,8,640]{3,2,0,1:T(8,128)(2,1)S(1)}, bf16[4,2,8,640]{3,2,0,1:T(8,128)(2,1)S(1)}, u32[]{:S(2)}, u32[]{:S(2)}) collective-permute-start(bf16[4,2,8,640]{3,2,0,1:T(8,128)(2,1)S(1)} %pad_maximum_fusion.5), channel_id=1, source_target_pairs={{0,1},{1,0},{2,3},{3,2},{4,5},{5,4},{6,7},{7,6},{8,9},{9,8},{10,11... | collective-permute-start | bytes 245768 | tf_op jit(solution)/shard_map/ppermute | solution.py:287
  14.7 1.0 %collective-permute-done.6 = bf16[4,8,768]{2,1,0:T(8,128)(2,1)S(1)} collective-permute-done((bf16[4,8,768]{2,1,0:T(8,128)(2,1)S(1)}, bf16[4,8,768]{2,1,0:T(8,128)(2,1)S(1)}, u32[]{:S(2)}, u32[]{:S(2)}) %collective-permute-start.6) | collective-permute-done | bytes 49184 | tf_op jit(solution)/shard_map/ppermute | solution.py:287
  15.8 1.6 %collective-permute-start.7 = (bf16[4,2,8,768]{3,2,0,1:T(8,128)(2,1)S(1)}, bf16[4,2,8,768]{3,2,0,1:T(8,128)(2,1)S(1)}, u32[]{:S(2)}, u32[]{:S(2)}) collective-permute-start(bf16[4,2,8,768]{3,2,0,1:T(8,128)(2,1)S(1)} %pad_maximum_fusion.4), channel_id=1, source_target_pairs={{0,2},{1,3},{2,0},{3,1},{4,6},{5,7},{6,4},{7,5},{8,10},{9,11},{10,... | collective-permute-start | bytes 294920 | tf_op jit(solution)/shard_map/ppermute | solution.py:287
  17.7 2.1 %collective-permute-start.5 = (bf16[4,2,2,8,640]{4,3,0,1,2:T(8,128)(2,1)S(1)}, bf16[4,2,2,8,640]{4,3,0,1,2:T(8,128)(2,1)S(1)}, u32[]{:S(2)}, u32[]{:S(2)}) collective-permute-start(bf16[4,2,2,8,640]{4,3,0,1,2:T(8,128)(2,1)S(1)} %pad_maximum_fusion.3), channel_id=1, source_target_pairs={{0,2},{1,3},{2,0},{3,1},{4,6},{5,7},{6,4},{7,5},{8,10},{9,11},{10,... | collective-permute-start | bytes 491528 | tf_op jit(solution)/shard_map/ppermute | solution.py:287
  19.8 1.0 %collective-permute-done.7 = bf16[4,2,8,768]{3,2,0,1:T(8,128)(2,1)S(1)} collective-permute-done((bf16[4,2,8,768]{3,2,0,1:T(8,128)(2,1)S(1)}, bf16[4,2,8,768]{3,2,0,1:T(8,128)(2,1)S(1)}, u32[]{:S(2)}, u32[]{:S(2)}) %collective-permute-start.7) | collective-permute-done | bytes 98336 | tf_op jit(solution)/shard_map/ppermute | solution.py:287
  20.9 1.6 %collective-permute-start.8 = (bf16[4,2,2,8,768]{4,3,0,1,2:T(8,128)(2,1)S(1)}, bf16[4,2,2,8,768]{4,3,0,1,2:T(8,128)(2,1)S(1)}, u32[]{:S(2)}, u32[]{:S(2)}) collective-permute-start(bf16[4,2,2,8,768]{4,3,0,1,2:T(8,128)(2,1)S(1)} %pad_maximum_fusion.2), channel_id=1, source_target_pairs={{0,1},{1,0},{2,3},{3,2},{4,5},{5,4},{6,7},{7,6},{8,9},{9,8},{10,11... | collective-permute-start | bytes 589832 | tf_op jit(solution)/shard_map/ppermute | solution.py:287
  22.5 0.6 %collective-permute-done.5 = bf16[4,2,2,8,640]{4,3,0,1,2:T(8,128)(2,1)S(1)} collective-permute-done((bf16[4,2,2,8,640]{4,3,0,1,2:T(8,128)(2,1)S(1)}, bf16[4,2,2,8,640]{4,3,0,1,2:T(8,128)(2,1)S(1)}, u32[]{:S(2)}, u32[]{:S(2)}) %collective-permute-start.5) | collective-permute-done | bytes 163872 | tf_op jit(solution)/shard_map/ppermute | solution.py:287
  23.1 3.7 %collective-permute-done.8 = bf16[4,2,2,8,768]{4,3,0,1,2:T(8,128)(2,1)S(1)} collective-permute-done((bf16[4,2,2,8,768]{4,3,0,1,2:T(8,128)(2,1)S(1)}, bf16[4,2,2,8,768]{4,3,0,1,2:T(8,128)(2,1)S(1)}, u32[]{:S(2)}, u32[]{:S(2)}) %collective-permute-start.8) | collective-permute-done | bytes 196640 | tf_op jit(solution)/shard_map/ppermute | solution.py:287
  26.9 0.8 %stats.1 = (f32[2,8,256]{2,1,0:T(8,128)S(1)}, f32[5,128,256]{2,1,0:T(8,128)S(1)}, f32[8,256]{1,0:T(8,128)S(1)}, bf16[256,128]{1,0:T(8,128)(2,1)S(1)}) custom-call(s32[8,128]{1,0:T(8,128)S(1)} %get-tuple-element.24.start_ref, bf16[256,768]{1,0:T(8,128)(2,1)S(1)} %bitcast.40, bf16[128,640]{1,0:T(8,128)(2,1)S(1)} %get-tuple-element.22.k_ref), custom_call_target="tpu_custom_call" | custom-call | tf_op jit(solution)/shard_map/stats/pallas_call | solution.py:166
  27.7 1.6 %collective-permute-start.9 = (f32[2,8,256]{2,1,0:T(8,128)S(1)}, f32[2,8,256]{2,1,0:T(8,128)S(1)}, u32[]{:S(2)}, u32[]{:S(2)}) collective-permute-start(f32[2,8,256]{2,1,0:T(8,128)S(1)} %get-tuple-element.30.own_ref), channel_id=1, source_target_pairs={{0,1},{1,0},{2,3},{3,2},{4,5},{5,4},{6,7},{7,6},{8,9},{9,8},{10,11... | collective-permute-start | bytes 49160 | tf_op jit(solution)/shard_map/ppermute | solution.py:287
  29.4 1.4 %query_gradients.1 = (bf16[256,768]{1,0:T(8,128)(2,1)}, bf16[5,128,256]{2,1,0:T(8,128)(2,1)S(1)}) custom-call(bf16[256,640]{1,0:T(8,128)(2,1)S(1)} %bitcast.42, bf16[128,640]{1,0:T(8,128)(2,1)S(1)} %get-tuple-element.22.k_ref, bf16[128,640]{1,0:T(8,128)(2,1)S(1)} %get-tuple-element.23.v_ref, f32[5,128,256]{2,1,0:T(8,128)S(1)} %get-tuple-element.25.p_ref, ...), custom_call_target="tpu_custom_call" | custom-call | tf_op jit(solution)/shard_map/query_gradients/pallas_call | solution.py:205
  30.8 4.2 %all-to-all-start = ((bf16[32,8,768]{2,1,0:T(8,128)(2,1)}), bf16[32,8,768]{2,1,0:T(8,128)(2,1)S(1)}, u32[]{:S(2)}, u32[]{:S(2)}) async-start(bf16[32,8,768]{2,1,0:T(8,128)(2,1)} %bitcast.45), calls=%async_computation | async-start | bytes 786432 | tf_op jit(solution)/shard_map/all_to_all | solution.py:323
  35.0 2.7 %collective-permute-start.10 = (f32[2,8,256]{2,1,0:T(8,128)S(1)}, f32[2,8,256]{2,1,0:T(8,128)S(1)}, u32[]{:S(2)}, u32[]{:S(2)}) collective-permute-start(f32[2,8,256]{2,1,0:T(8,128)S(1)} %pad_maximum_fusion.10), channel_id=1, source_target_pairs={{0,4},{1,5},{2,6},{3,7},{4,0},{5,1},{6,2},{7,3},{8,12},{9,13},{10,... | collective-permute-start | bytes 49160 | tf_op jit(solution)/shard_map/ppermute | solution.py:287
  37.7 10.1 %collective-permute-done.10 = f32[2,8,256]{2,1,0:T(8,128)S(1)} collective-permute-done((f32[2,8,256]{2,1,0:T(8,128)S(1)}, f32[2,8,256]{2,1,0:T(8,128)S(1)}, u32[]{:S(2)}, u32[]{:S(2)}) %collective-permute-start.10) | collective-permute-done | bytes 16416 | tf_op jit(solution)/shard_map/ppermute | solution.py:287
  47.9 3.7 %collective-permute-done.11 = f32[2,8,256]{2,1,0:T(8,128)S(1)} collective-permute-done((f32[2,8,256]{2,1,0:T(8,128)S(1)}, f32[2,8,256]{2,1,0:T(8,128)S(1)}, u32[]{:S(2)}, u32[]{:S(2)}) %collective-permute-start.11) | collective-permute-done | bytes 16416 | tf_op jit(solution)/shard_map/ppermute | solution.py:287
  51.7 1.0 %cache_gradients.1 = (bf16[128,640]{1,0:T(8,128)(2,1)}, bf16[128,640]{1,0:T(8,128)(2,1)}) custom-call(bf16[256,768]{1,0:T(8,128)(2,1)S(1)} %bitcast.41, bf16[256,640]{1,0:T(8,128)(2,1)S(1)} %bitcast.43, f32[5,128,256]{2,1,0:T(8,128)S(1)} %get-tuple-element.25.p_ref, bf16[5,128,256]{2,1,0:T(8,128)(2,1)S(1)} %get-tuple-element.29.ds_ref, ...), custom_call_target="tpu_custom_call" | custom-call | tf_op jit(solution)/shard_map/cache_gradients/pallas_call | solution.py:235
  52.7 1.0 %combine.1 = bf16[8,2560]{1,0:T(8,128)(2,1)} custom-call(bf16[256,768]{1,0:T(8,128)(2,1)S(1)} %bitcast.44), custom_call_target="tpu_custom_call" | custom-call | tf_op jit(solution)/shard_map/combine/pallas_call | solution.py:267
  (30 shorter events, 1.1 us)
Async XLA Ops:
  1.8 4.0 %collective-permute-start = (bf16[8,1408]{1,0:T(8,128)(2,1)S(1)}, bf16[8,1408]{1,0:T(8,128)(2,1)S(1)}, u32[]{:S(2)}, u32[]{:S(2)}) collective-permute-start(bf16[8,1408]{1,0:T(8,128)(2,1)S(1)} %get-tuple-element.18), channel_id=1, source_target_pairs={{0,24},{8,16},{16,8},{24,0},{1,25},{9,17},{17,9},{25,1},{2,26},{10... | collective-permute-start | bytes 67592 | tf_op jit(solution)/shard_map/ppermute | solution.py:287
  4.2 3.8 %collective-permute-start.1 = (bf16[8,1408]{1,0:T(8,128)(2,1)S(1)}, bf16[8,1408]{1,0:T(8,128)(2,1)S(1)}, u32[]{:S(2)}, u32[]{:S(2)}) collective-permute-start(bf16[8,1408]{1,0:T(8,128)(2,1)S(1)} %get-tuple-element.19), channel_id=1, source_target_pairs={{0,16},{8,24},{16,0},{24,8},{1,17},{9,25},{17,1},{25,9},{2,18},{10... | collective-permute-start | bytes 67592 | tf_op jit(solution)/shard_map/ppermute | solution.py:287
  4.9 3.2 %collective-permute-start.2 = (bf16[8,1408]{1,0:T(8,128)(2,1)S(1)}, bf16[8,1408]{1,0:T(8,128)(2,1)S(1)}, u32[]{:S(2)}, u32[]{:S(2)}) collective-permute-start(bf16[8,1408]{1,0:T(8,128)(2,1)S(1)} %get-tuple-element.20), channel_id=1, source_target_pairs={{0,8},{8,0},{16,24},{24,16},{1,9},{9,1},{17,25},{25,17},{2,10},{10... | collective-permute-start | bytes 67592 | tf_op jit(solution)/shard_map/ppermute | solution.py:287
  8.1 5.0 %collective-permute-start.3 = (bf16[4,8,640]{2,1,0:T(8,128)(2,1)S(1)}, bf16[4,8,640]{2,1,0:T(8,128)(2,1)S(1)}, u32[]{:S(2)}, u32[]{:S(2)}) collective-permute-start(bf16[4,8,640]{2,1,0:T(8,128)(2,1)S(1)} %pad_maximum_fusion.9), channel_id=1, source_target_pairs={{0,4},{1,5},{2,6},{3,7},{4,0},{5,1},{6,2},{7,3},{8,12},{9,13},{10,... | collective-permute-start | bytes 122888 | tf_op jit(solution)/shard_map/ppermute | solution.py:287
  10.7 5.0 %collective-permute-start.6 = (bf16[4,8,768]{2,1,0:T(8,128)(2,1)S(1)}, bf16[4,8,768]{2,1,0:T(8,128)(2,1)S(1)}, u32[]{:S(2)}, u32[]{:S(2)}) collective-permute-start(bf16[4,8,768]{2,1,0:T(8,128)(2,1)S(1)} %pad_maximum_fusion.6), channel_id=1, source_target_pairs={{0,4},{1,5},{2,6},{3,7},{4,0},{5,1},{6,2},{7,3},{8,12},{9,13},{10,... | collective-permute-start | bytes 147464 | tf_op jit(solution)/shard_map/ppermute | solution.py:287
  13.1 4.5 %collective-permute-start.4 = (bf16[4,2,8,640]{3,2,0,1:T(8,128)(2,1)S(1)}, bf16[4,2,8,640]{3,2,0,1:T(8,128)(2,1)S(1)}, u32[]{:S(2)}, u32[]{:S(2)}) collective-permute-start(bf16[4,2,8,640]{3,2,0,1:T(8,128)(2,1)S(1)} %pad_maximum_fusion.5), channel_id=1, source_target_pairs={{0,1},{1,0},{2,3},{3,2},{4,5},{5,4},{6,7},{7,6},{8,9},{9,8},{10,11... | collective-permute-start | bytes 245768 | tf_op jit(solution)/shard_map/ppermute | solution.py:287
  15.8 5.1 %collective-permute-start.7 = (bf16[4,2,8,768]{3,2,0,1:T(8,128)(2,1)S(1)}, bf16[4,2,8,768]{3,2,0,1:T(8,128)(2,1)S(1)}, u32[]{:S(2)}, u32[]{:S(2)}) collective-permute-start(bf16[4,2,8,768]{3,2,0,1:T(8,128)(2,1)S(1)} %pad_maximum_fusion.4), channel_id=1, source_target_pairs={{0,2},{1,3},{2,0},{3,1},{4,6},{5,7},{6,4},{7,5},{8,10},{9,11},{10,... | collective-permute-start | bytes 294920 | tf_op jit(solution)/shard_map/ppermute | solution.py:287
  17.7 5.4 %collective-permute-start.5 = (bf16[4,2,2,8,640]{4,3,0,1,2:T(8,128)(2,1)S(1)}, bf16[4,2,2,8,640]{4,3,0,1,2:T(8,128)(2,1)S(1)}, u32[]{:S(2)}, u32[]{:S(2)}) collective-permute-start(bf16[4,2,2,8,640]{4,3,0,1,2:T(8,128)(2,1)S(1)} %pad_maximum_fusion.3), channel_id=1, source_target_pairs={{0,2},{1,3},{2,0},{3,1},{4,6},{5,7},{6,4},{7,5},{8,10},{9,11},{10,... | collective-permute-start | bytes 491528 | tf_op jit(solution)/shard_map/ppermute | solution.py:287
  20.9 5.9 %collective-permute-start.8 = (bf16[4,2,2,8,768]{4,3,0,1,2:T(8,128)(2,1)S(1)}, bf16[4,2,2,8,768]{4,3,0,1,2:T(8,128)(2,1)S(1)}, u32[]{:S(2)}, u32[]{:S(2)}) collective-permute-start(bf16[4,2,2,8,768]{4,3,0,1,2:T(8,128)(2,1)S(1)} %pad_maximum_fusion.2), channel_id=1, source_target_pairs={{0,1},{1,0},{2,3},{3,2},{4,5},{5,4},{6,7},{7,6},{8,9},{9,8},{10,11... | collective-permute-start | bytes 589832 | tf_op jit(solution)/shard_map/ppermute | solution.py:287
  27.7 7.3 %collective-permute-start.9 = (f32[2,8,256]{2,1,0:T(8,128)S(1)}, f32[2,8,256]{2,1,0:T(8,128)S(1)}, u32[]{:S(2)}, u32[]{:S(2)}) collective-permute-start(f32[2,8,256]{2,1,0:T(8,128)S(1)} %get-tuple-element.30.own_ref), channel_id=1, source_target_pairs={{0,1},{1,0},{2,3},{3,2},{4,5},{5,4},{6,7},{7,6},{8,9},{9,8},{10,11... | collective-permute-start | bytes 49160 | tf_op jit(solution)/shard_map/ppermute | solution.py:287
  30.8 22.0 %all-to-all-start = ((bf16[32,8,768]{2,1,0:T(8,128)(2,1)}), bf16[32,8,768]{2,1,0:T(8,128)(2,1)S(1)}, u32[]{:S(2)}, u32[]{:S(2)}) async-start(bf16[32,8,768]{2,1,0:T(8,128)(2,1)} %bitcast.45), calls=%async_computation | async-start | bytes 786432 | tf_op jit(solution)/shard_map/all_to_all | solution.py:323
  35.0 12.8 %collective-permute-start.10 = (f32[2,8,256]{2,1,0:T(8,128)S(1)}, f32[2,8,256]{2,1,0:T(8,128)S(1)}, u32[]{:S(2)}, u32[]{:S(2)}) collective-permute-start(f32[2,8,256]{2,1,0:T(8,128)S(1)} %pad_maximum_fusion.10), channel_id=1, source_target_pairs={{0,4},{1,5},{2,6},{3,7},{4,0},{5,1},{6,2},{7,3},{8,12},{9,13},{10,... | collective-permute-start | bytes 49160 | tf_op jit(solution)/shard_map/ppermute | solution.py:287
  47.9 3.8 %collective-permute-start.11 = (f32[2,8,256]{2,1,0:T(8,128)S(1)}, f32[2,8,256]{2,1,0:T(8,128)S(1)}, u32[]{:S(2)}, u32[]{:S(2)}) collective-permute-start(f32[2,8,256]{2,1,0:T(8,128)S(1)} %pad_maximum_fusion.11), channel_id=1, source_target_pairs={{0,2},{1,3},{2,0},{3,1},{4,6},{5,7},{6,4},{7,5},{8,10},{9,11},{10,... | collective-permute-start | bytes 49160 | tf_op jit(solution)/shard_map/ppermute | solution.py:287

commit v4 on v3

--- a/solution.py
+++ b/solution.py
@@ -140,7 +140,7 @@
     slots = -(-heads // 8) * 8
     scaling = HEAD_DIM ** (-0.5)
 
-    def body(start_ref, q_ref, k_ref, out_ref, prob_ref, delta_ref, sent_ref):
+    def body(start_ref, q_ref, k_ref, out_ref, prob_ref):
         visible = visible_of(start_ref, (key_count, m), row_count, key_total)
         out_ref[...] = jnp.ones_like(out_ref)
         for h in range(heads):
@@ -151,56 +151,53 @@
             prob_ref[h] = prob
             out_ref[0, pl.ds(h, 1), :] = top
             out_ref[1, pl.ds(h, 1), :] = jnp.sum(prob, axis=0, keepdims=True)
-        slot = lax.broadcasted_iota(jnp.int32, (slots, LANES), 0)
-        lane = lax.broadcasted_iota(jnp.int32, (slots, LANES), 1)
-        pick = (lane % heads == slot) & (lane < 3 * heads)
-        delta_ref[...] = nt(jnp.where(pick, 1.0, 0.0).astype(BF), q_ref[:, pl.ds(here, LANES)])
-        sent = jnp.zeros((m, LANES), F32)
-        for i in range(2):
-            for part, value in enumerate(split3(out_ref[i])):
-                at = (3 * i + part) * heads
-                place = (lane == at + slot) & (slot < heads)
-                sent += tn(value, jnp.where(place, 1.0, 0.0).astype(BF))
-        sent_ref[...] = sent.astype(BF)
 
     return pl.pallas_call(
         body,
         in_specs=in_vmem(3),
-        out_specs=in_vmem(4),
+        out_specs=in_vmem(2),
         out_shape=[
             held((2, slots, m), F32),
             held((heads, key_count, m), F32),
-            held((slots, m), F32),
-            held((m, LANES), BF),
         ],
         name="stats",
     )(vmem(start), vmem(queries), vmem(keys))
 
 
-def query_kernel(grads, keys, values, probs, deltas, sent):
+def query_kernel(queries, grads, keys, values, probs, own):
     m = grads.shape[0]
     key_count, here = keys.shape
     heads = here // HEAD_DIM
+    slots = own.shape[1]
     scaling = HEAD_DIM ** (-0.5)
 
-    def body(g_ref, k_ref, v_ref, p_ref, d_ref, sent_ref, u_hbm, ds_ref, u_ref, sems):
+    def body(q_ref, g_ref, k_ref, v_ref, p_ref, own_ref, u_hbm, ds_ref, u_ref, sems):
         def copy_of(h):
             return pltpu.make_async_copy(
                 u_ref.at[:, head_of(h)], u_hbm.at[:, head_of(h)], sems.at[h]
             )
 
-        last = pltpu.make_async_copy(sent_ref, u_hbm.at[:, head_of(heads)], sems.at[heads])
-        last.start()
+        slot = lax.broadcasted_iota(jnp.int32, (slots, LANES), 0)
+        lane = lax.broadcasted_iota(jnp.int32, (slots, LANES), 1)
+        pick = (lane % heads == slot) & (lane < 3 * heads)
+        deltas = nt(jnp.where(pick, 1.0, 0.0).astype(BF), q_ref[:, pl.ds(here, LANES)])
+        sent = jnp.zeros((m, LANES), F32)
+        for i in range(2):
+            for part, value in enumerate(split3(own_ref[i])):
+                at = (3 * i + part) * heads
+                place = (lane == at + slot) & (slot < heads)
+                sent += tn(value, jnp.where(place, 1.0, 0.0).astype(BF))
+        u_ref[:, head_of(heads)] = sent.astype(BF)
+        copy_of(heads).start()
         for h in range(heads):
             at = head_of(h)
-            ds = p_ref[h] * (nt(v_ref[:, at], g_ref[:, at]) - d_ref[h : h + 1, :]) * scaling
+            ds = p_ref[h] * (nt(v_ref[:, at], g_ref[:, at]) - deltas[h : h + 1, :]) * scaling
             ds = ds.astype(BF)
             u_ref[:, at] = tn(ds, k_ref[:, at]).astype(BF)
             copy_of(h).start()
             ds_ref[h] = ds
-        for h in range(heads):
+        for h in range(heads + 1):
             copy_of(h).wait()
-        last.wait()
 
     return pl.pallas_call(
         body,
@@ -211,11 +208,11 @@
             held((heads, key_count, m), BF),
         ],
         scratch_shapes=[
-            pltpu.VMEM((m, here), BF),
+            pltpu.VMEM((m, here + LANES), BF),
             pltpu.SemaphoreType.DMA((heads + 1,)),
         ],
         name="query_gradients",
-    )(vmem(grads), vmem(keys), vmem(values), vmem(probs), vmem(deltas), vmem(sent))
+    )(vmem(queries), vmem(grads), vmem(keys), vmem(values), vmem(probs), vmem(own))
 
 
 def cache_kernel(queries, grads, probs, score_grads, own, merged):
@@ -355,9 +352,9 @@
     grad_all = spread_blocks(grad_all, "ctx", down[:1] + down[1:][::-1])
     grad_all = grad_all.reshape(peers * rows, here)
 
-    own, probs, deltas, row_stats = stats_kernel(start, query_all, keys, row_count, key_total)
+    own, probs = stats_kernel(start, query_all, keys, row_count, key_total)
     merged = merge_stats(own, "ctx", down[-1:] + down[:-1])
-    part, score_grads = query_kernel(grad_all, keys, values, probs, deltas, row_stats)
+    part, score_grads = query_kernel(query_all, grad_all, keys, values, probs, own)
     part = exchange(part.reshape(peers, rows, here + LANES))
     grad_keys, grad_values = cache_kernel(query_all, grad_all, probs, score_grads, own, merged)
     part = part.reshape(peers * rows, here + LANES)

time: 54 us -> 53.9 us (level)
  no operation moved by 1% of the time
where the time goes in v4:
time: 53.9 us; the launch traced here: 53.7 us
  waiting for transfers between devices  25.5 us (47%)
  starting transfers between devices  21.7 us (40%)
  Pallas kernels  5.22 us (10%)
  between operations  0.82 us (2%)
    ppermute x12, waiting for transfers between devices, flip(): return lax.ppermute(value, axis, [(i, i ^ bit) for i in range(count)])  25.5 us
    ppermute x12, starting transfers between devices, flip(): return lax.ppermute(value, axis, [(i, i ^ bit) for i in range(count)])  17.5 us
    all_to_all x1, starting transfers between devices, exchange(): return lax.all_to_all(blocks, ('section', 'ctx'), 0, 0, tiled=True)  4.19 us
    pallas_call x1, Pallas kernels, query_kernel(): pl.pallas_call(body, in_specs=in_vmem(6), out_specs=[pl.BlockSpec(memory_...  1.65 us
    pallas_call x1, Pallas kernels, pack(): pl.pallas_call(body, in_specs=[pl.BlockSpec(memory_space=pl.ANY)] * 6, ou...  1.12 us
  transfers between devices with their start and end apart: 13, of which 10 were waited for; matrix products, arithmetic and copies ran while one was open for 1% of the time, Pallas kernels for 5%

profile of v4, /device:TPU:0, one launch (start us, length us, event | category | flops | bytes accessed | tf_op | source)
XLA Modules:
  0.0 53.7 jit_solution(11322731812405291917)
XLA Ops:
  0.6 1.1 %pack.1 = (bf16[8,1408]{1,0:T(8,128)(2,1)S(1)}, bf16[8,1408]{1,0:T(8,128)(2,1)S(1)}, bf16[8,1408]{1,0:T(8,128)(2,1)S(1)}, bf16[8,1408]{1,0:T(8,128)(2,1)S(1)}, s...) custom-call(s32[8]{0:T(128)} %order_hbm.1, bf16[128,640]{1,0:T(8,128)(2,1)} %k_hbm.1, ...), custom_call_target="tpu_custom_call" | custom-call | tf_op jit(solution)/shard_map/pack/pallas_call | solution.py:109
  1.8 2.5 %collective-permute-start = (bf16[8,1408]{1,0:T(8,128)(2,1)S(1)}, bf16[8,1408]{1,0:T(8,128)(2,1)S(1)}, u32[]{:S(2)}, u32[]{:S(2)}) collective-permute-start(bf16[8,1408]{1,0:T(8,128)(2,1)S(1)} %get-tuple-element.16), channel_id=1, source_target_pairs={{0,24},{8,16},{16,8},{24,0},{1,25},{9,17},{17,9},{25,1},{2,26},{10... | collective-permute-start | bytes 67592 | tf_op jit(solution)/shard_map/ppermute | solution.py:284
  4.2 0.6 %collective-permute-start.1 = (bf16[8,1408]{1,0:T(8,128)(2,1)S(1)}, bf16[8,1408]{1,0:T(8,128)(2,1)S(1)}, u32[]{:S(2)}, u32[]{:S(2)}) collective-permute-start(bf16[8,1408]{1,0:T(8,128)(2,1)S(1)} %get-tuple-element.17), channel_id=1, source_target_pairs={{0,16},{8,24},{16,0},{24,8},{1,17},{9,25},{17,1},{25,9},{2,18},{10... | collective-permute-start | bytes 67592 | tf_op jit(solution)/shard_map/ppermute | solution.py:284
  4.9 0.9 %collective-permute-done = bf16[8,1408]{1,0:T(8,128)(2,1)S(1)} collective-permute-done((bf16[8,1408]{1,0:T(8,128)(2,1)S(1)}, bf16[8,1408]{1,0:T(8,128)(2,1)S(1)}, u32[]{:S(2)}, u32[]{:S(2)}) %collective-permute-start) | collective-permute-done | bytes 22560 | tf_op jit(solution)/shard_map/ppermute | solution.py:284
  5.8 2.2 %collective-permute-done.1 = bf16[8,1408]{1,0:T(8,128)(2,1)S(1)} collective-permute-done((bf16[8,1408]{1,0:T(8,128)(2,1)S(1)}, bf16[8,1408]{1,0:T(8,128)(2,1)S(1)}, u32[]{:S(2)}, u32[]{:S(2)}) %collective-permute-start.1) | collective-permute-done | bytes 22560 | tf_op jit(solution)/shard_map/ppermute | solution.py:284
  8.1 2.7 %collective-permute-start.6 = (bf16[4,8,640]{2,1,0:T(8,128)(2,1)S(1)}, bf16[4,8,640]{2,1,0:T(8,128)(2,1)S(1)}, u32[]{:S(2)}, u32[]{:S(2)}) collective-permute-start(bf16[4,8,640]{2,1,0:T(8,128)(2,1)S(1)} %pad_maximum_fusion.7), channel_id=1, source_target_pairs={{0,4},{1,5},{2,6},{3,7},{4,0},{5,1},{6,2},{7,3},{8,12},{9,13},{10,... | collective-permute-start | bytes 122888 | tf_op jit(solution)/shard_map/ppermute | solution.py:284
  11.2 1.9 %collective-permute-done.6 = bf16[4,8,640]{2,1,0:T(8,128)(2,1)S(1)} collective-permute-done((bf16[4,8,640]{2,1,0:T(8,128)(2,1)S(1)}, bf16[4,8,640]{2,1,0:T(8,128)(2,1)S(1)}, u32[]{:S(2)}, u32[]{:S(2)}) %collective-permute-start.6) | collective-permute-done | bytes 40992 | tf_op jit(solution)/shard_map/ppermute | solution.py:284
  13.1 1.6 %collective-permute-start.7 = (bf16[4,2,8,640]{3,2,0,1:T(8,128)(2,1)S(1)}, bf16[4,2,8,640]{3,2,0,1:T(8,128)(2,1)S(1)}, u32[]{:S(2)}, u32[]{:S(2)}) collective-permute-start(bf16[4,2,8,640]{3,2,0,1:T(8,128)(2,1)S(1)} %pad_maximum_fusion.6), channel_id=1, source_target_pairs={{0,1},{1,0},{2,3},{3,2},{4,5},{5,4},{6,7},{7,6},{8,9},{9,8},{10,11... | collective-permute-start | bytes 245768 | tf_op jit(solution)/shard_map/ppermute | solution.py:284
  14.7 1.1 %collective-permute-done.3 = bf16[4,8,768]{2,1,0:T(8,128)(2,1)S(1)} collective-permute-done((bf16[4,8,768]{2,1,0:T(8,128)(2,1)S(1)}, bf16[4,8,768]{2,1,0:T(8,128)(2,1)S(1)}, u32[]{:S(2)}, u32[]{:S(2)}) %collective-permute-start.3) | collective-permute-done | bytes 49184 | tf_op jit(solution)/shard_map/ppermute | solution.py:284
  15.9 1.6 %collective-permute-start.4 = (bf16[4,2,8,768]{3,2,0,1:T(8,128)(2,1)S(1)}, bf16[4,2,8,768]{3,2,0,1:T(8,128)(2,1)S(1)}, u32[]{:S(2)}, u32[]{:S(2)}) collective-permute-start(bf16[4,2,8,768]{3,2,0,1:T(8,128)(2,1)S(1)} %pad_maximum_fusion.4), channel_id=1, source_target_pairs={{0,2},{1,3},{2,0},{3,1},{4,6},{5,7},{6,4},{7,5},{8,10},{9,11},{10,... | collective-permute-start | bytes 294920 | tf_op jit(solution)/shard_map/ppermute | solution.py:284
  17.7 2.1 %collective-permute-start.8 = (bf16[4,2,2,8,640]{4,3,0,1,2:T(8,128)(2,1)S(1)}, bf16[4,2,2,8,640]{4,3,0,1,2:T(8,128)(2,1)S(1)}, u32[]{:S(2)}, u32[]{:S(2)}) collective-permute-start(bf16[4,2,2,8,640]{4,3,0,1,2:T(8,128)(2,1)S(1)} %pad_maximum_fusion.3), channel_id=1, source_target_pairs={{0,2},{1,3},{2,0},{3,1},{4,6},{5,7},{6,4},{7,5},{8,10},{9,11},{10,... | collective-permute-start | bytes 491528 | tf_op jit(solution)/shard_map/ppermute | solution.py:284
  19.8 1.1 %collective-permute-done.4 = bf16[4,2,8,768]{3,2,0,1:T(8,128)(2,1)S(1)} collective-permute-done((bf16[4,2,8,768]{3,2,0,1:T(8,128)(2,1)S(1)}, bf16[4,2,8,768]{3,2,0,1:T(8,128)(2,1)S(1)}, u32[]{:S(2)}, u32[]{:S(2)}) %collective-permute-start.4) | collective-permute-done | bytes 98336 | tf_op jit(solution)/shard_map/ppermute | solution.py:284
  21.0 1.6 %collective-permute-start.5 = (bf16[4,2,2,8,768]{4,3,0,1,2:T(8,128)(2,1)S(1)}, bf16[4,2,2,8,768]{4,3,0,1,2:T(8,128)(2,1)S(1)}, u32[]{:S(2)}, u32[]{:S(2)}) collective-permute-start(bf16[4,2,2,8,768]{4,3,0,1,2:T(8,128)(2,1)S(1)} %pad_maximum_fusion.2), channel_id=1, source_target_pairs={{0,1},{1,0},{2,3},{3,2},{4,5},{5,4},{6,7},{7,6},{8,9},{9,8},{10,11... | collective-permute-start | bytes 589832 | tf_op jit(solution)/shard_map/ppermute | solution.py:284
  22.6 0.5 collective-permute-done.8
  23.1 3.7 %collective-permute-done.5 = bf16[4,2,2,8,768]{4,3,0,1,2:T(8,128)(2,1)S(1)} collective-permute-done((bf16[4,2,2,8,768]{4,3,0,1,2:T(8,128)(2,1)S(1)}, bf16[4,2,2,8,768]{4,3,0,1,2:T(8,128)(2,1)S(1)}, u32[]{:S(2)}, u32[]{:S(2)}) %collective-permute-start.5) | collective-permute-done | bytes 196640 | tf_op jit(solution)/shard_map/ppermute | solution.py:284
  27.0 0.4 stats.1
  27.4 1.6 %collective-permute-start.9 = (f32[2,8,256]{2,1,0:T(8,128)S(1)}, f32[2,8,256]{2,1,0:T(8,128)S(1)}, u32[]{:S(2)}, u32[]{:S(2)}) collective-permute-start(f32[2,8,256]{2,1,0:T(8,128)S(1)} %get-tuple-element.24.own_ref), channel_id=1, source_target_pairs={{0,1},{1,0},{2,3},{3,2},{4,5},{5,4},{6,7},{7,6},{8,9},{9,8},{10,11... | collective-permute-start | bytes 49160 | tf_op jit(solution)/shard_map/ppermute | solution.py:284
  29.1 1.7 %query_gradients.1 = (bf16[256,768]{1,0:T(8,128)(2,1)}, bf16[5,128,256]{2,1,0:T(8,128)(2,1)S(1)}) custom-call(bf16[256,768]{1,0:T(8,128)(2,1)S(1)} %bitcast.41, bf16[256,640]{1,0:T(8,128)(2,1)S(1)} %bitcast.43, bf16[128,640]{1,0:T(8,128)(2,1)S(1)} %get-tuple-element.20.k_ref, bf16[128,640]{1,0:T(8,128)(2,1)S(1)} %get-tuple-element.21.v_ref, ...), custom_call_target="tpu_custom_call" | custom-call | tf_op jit(solution)/shard_map/query_gradients/pallas_call | solution.py:202
  30.7 4.2 %all-to-all-start = ((bf16[32,8,768]{2,1,0:T(8,128)(2,1)}), bf16[32,8,768]{2,1,0:T(8,128)(2,1)S(1)}, u32[]{:S(2)}, u32[]{:S(2)}) async-start(bf16[32,8,768]{2,1,0:T(8,128)(2,1)} %bitcast.46), calls=%async_computation | async-start | bytes 786432 | tf_op jit(solution)/shard_map/all_to_all | solution.py:320
  35.0 2.7 %collective-permute-start.10 = (f32[2,8,256]{2,1,0:T(8,128)S(1)}, f32[2,8,256]{2,1,0:T(8,128)S(1)}, u32[]{:S(2)}, u32[]{:S(2)}) collective-permute-start(f32[2,8,256]{2,1,0:T(8,128)S(1)} %pad_maximum_fusion.8), channel_id=1, source_target_pairs={{0,4},{1,5},{2,6},{3,7},{4,0},{5,1},{6,2},{7,3},{8,12},{9,13},{10,... | collective-permute-start | bytes 49160 | tf_op jit(solution)/shard_map/ppermute | solution.py:284
  37.7 10.1 %collective-permute-done.10 = f32[2,8,256]{2,1,0:T(8,128)S(1)} collective-permute-done((f32[2,8,256]{2,1,0:T(8,128)S(1)}, f32[2,8,256]{2,1,0:T(8,128)S(1)}, u32[]{:S(2)}, u32[]{:S(2)}) %collective-permute-start.10) | collective-permute-done | bytes 16416 | tf_op jit(solution)/shard_map/ppermute | solution.py:284
  47.9 3.7 %collective-permute-done.11 = f32[2,8,256]{2,1,0:T(8,128)S(1)} collective-permute-done((f32[2,8,256]{2,1,0:T(8,128)S(1)}, f32[2,8,256]{2,1,0:T(8,128)S(1)}, u32[]{:S(2)}, u32[]{:S(2)}) %collective-permute-start.11) | collective-permute-done | bytes 16416 | tf_op jit(solution)/shard_map/ppermute | solution.py:284
  51.7 1.0 %cache_gradients.1 = (bf16[128,640]{1,0:T(8,128)(2,1)}, bf16[128,640]{1,0:T(8,128)(2,1)}) custom-call(bf16[256,768]{1,0:T(8,128)(2,1)S(1)} %bitcast.42, bf16[256,640]{1,0:T(8,128)(2,1)S(1)} %bitcast.44, f32[5,128,256]{2,1,0:T(8,128)S(1)} %get-tuple-element.23.p_ref, bf16[5,128,256]{2,1,0:T(8,128)(2,1)S(1)} %get-tuple-element.26.ds_ref, ...), custom_call_target="tpu_custom_call" | custom-call | tf_op jit(solution)/shard_map/cache_gradients/pallas_call | solution.py:232
  52.7 1.0 %combine.1 = bf16[8,2560]{1,0:T(8,128)(2,1)} custom-call(bf16[256,768]{1,0:T(8,128)(2,1)S(1)} %bitcast.45), custom_call_target="tpu_custom_call" | custom-call | tf_op jit(solution)/shard_map/combine/pallas_call | solution.py:264
  (31 shorter events, 1.1 us)
Async XLA Ops:
  1.8 4.0 %collective-permute-start = (bf16[8,1408]{1,0:T(8,128)(2,1)S(1)}, bf16[8,1408]{1,0:T(8,128)(2,1)S(1)}, u32[]{:S(2)}, u32[]{:S(2)}) collective-permute-start(bf16[8,1408]{1,0:T(8,128)(2,1)S(1)} %get-tuple-element.16), channel_id=1, source_target_pairs={{0,24},{8,16},{16,8},{24,0},{1,25},{9,17},{17,9},{25,1},{2,26},{10... | collective-permute-start | bytes 67592 | tf_op jit(solution)/shard_map/ppermute | solution.py:284
  4.2 3.8 %collective-permute-start.1 = (bf16[8,1408]{1,0:T(8,128)(2,1)S(1)}, bf16[8,1408]{1,0:T(8,128)(2,1)S(1)}, u32[]{:S(2)}, u32[]{:S(2)}) collective-permute-start(bf16[8,1408]{1,0:T(8,128)(2,1)S(1)} %get-tuple-element.17), channel_id=1, source_target_pairs={{0,16},{8,24},{16,0},{24,8},{1,17},{9,25},{17,1},{25,9},{2,18},{10... | collective-permute-start | bytes 67592 | tf_op jit(solution)/shard_map/ppermute | solution.py:284
  4.9 3.2 %collective-permute-start.2 = (bf16[8,1408]{1,0:T(8,128)(2,1)S(1)}, bf16[8,1408]{1,0:T(8,128)(2,1)S(1)}, u32[]{:S(2)}, u32[]{:S(2)}) collective-permute-start(bf16[8,1408]{1,0:T(8,128)(2,1)S(1)} %get-tuple-element.18), channel_id=1, source_target_pairs={{0,8},{8,0},{16,24},{24,16},{1,9},{9,1},{17,25},{25,17},{2,10},{10... | collective-permute-start | bytes 67592 | tf_op jit(solution)/shard_map/ppermute | solution.py:284
  8.1 5.0 %collective-permute-start.6 = (bf16[4,8,640]{2,1,0:T(8,128)(2,1)S(1)}, bf16[4,8,640]{2,1,0:T(8,128)(2,1)S(1)}, u32[]{:S(2)}, u32[]{:S(2)}) collective-permute-start(bf16[4,8,640]{2,1,0:T(8,128)(2,1)S(1)} %pad_maximum_fusion.7), channel_id=1, source_target_pairs={{0,4},{1,5},{2,6},{3,7},{4,0},{5,1},{6,2},{7,3},{8,12},{9,13},{10,... | collective-permute-start | bytes 122888 | tf_op jit(solution)/shard_map/ppermute | solution.py:284
  10.8 5.1 %collective-permute-start.3 = (bf16[4,8,768]{2,1,0:T(8,128)(2,1)S(1)}, bf16[4,8,768]{2,1,0:T(8,128)(2,1)S(1)}, u32[]{:S(2)}, u32[]{:S(2)}) collective-permute-start(bf16[4,8,768]{2,1,0:T(8,128)(2,1)S(1)} %slice.44), channel_id=1, source_target_pairs={{0,4},{1,5},{2,6},{3,7},{4,0},{5,1},{6,2},{7,3},{8,12},{9,13},{10,... | collective-permute-start | bytes 147464 | tf_op jit(solution)/shard_map/ppermute | solution.py:284
  13.1 4.5 %collective-permute-start.7 = (bf16[4,2,8,640]{3,2,0,1:T(8,128)(2,1)S(1)}, bf16[4,2,8,640]{3,2,0,1:T(8,128)(2,1)S(1)}, u32[]{:S(2)}, u32[]{:S(2)}) collective-permute-start(bf16[4,2,8,640]{3,2,0,1:T(8,128)(2,1)S(1)} %pad_maximum_fusion.6), channel_id=1, source_target_pairs={{0,1},{1,0},{2,3},{3,2},{4,5},{5,4},{6,7},{7,6},{8,9},{9,8},{10,11... | collective-permute-start | bytes 245768 | tf_op jit(solution)/shard_map/ppermute | solution.py:284
  15.9 5.1 %collective-permute-start.4 = (bf16[4,2,8,768]{3,2,0,1:T(8,128)(2,1)S(1)}, bf16[4,2,8,768]{3,2,0,1:T(8,128)(2,1)S(1)}, u32[]{:S(2)}, u32[]{:S(2)}) collective-permute-start(bf16[4,2,8,768]{3,2,0,1:T(8,128)(2,1)S(1)} %pad_maximum_fusion.4), channel_id=1, source_target_pairs={{0,2},{1,3},{2,0},{3,1},{4,6},{5,7},{6,4},{7,5},{8,10},{9,11},{10,... | collective-permute-start | bytes 294920 | tf_op jit(solution)/shard_map/ppermute | solution.py:284
  17.7 5.4 %collective-permute-start.8 = (bf16[4,2,2,8,640]{4,3,0,1,2:T(8,128)(2,1)S(1)}, bf16[4,2,2,8,640]{4,3,0,1,2:T(8,128)(2,1)S(1)}, u32[]{:S(2)}, u32[]{:S(2)}) collective-permute-start(bf16[4,2,2,8,640]{4,3,0,1,2:T(8,128)(2,1)S(1)} %pad_maximum_fusion.3), channel_id=1, source_target_pairs={{0,2},{1,3},{2,0},{3,1},{4,6},{5,7},{6,4},{7,5},{8,10},{9,11},{10,... | collective-permute-start | bytes 491528 | tf_op jit(solution)/shard_map/ppermute | solution.py:284
  21.0 5.9 %collective-permute-start.5 = (bf16[4,2,2,8,768]{4,3,0,1,2:T(8,128)(2,1)S(1)}, bf16[4,2,2,8,768]{4,3,0,1,2:T(8,128)(2,1)S(1)}, u32[]{:S(2)}, u32[]{:S(2)}) collective-permute-start(bf16[4,2,2,8,768]{4,3,0,1,2:T(8,128)(2,1)S(1)} %pad_maximum_fusion.2), channel_id=1, source_target_pairs={{0,1},{1,0},{2,3},{3,2},{4,5},{5,4},{6,7},{7,6},{8,9},{9,8},{10,11... | collective-permute-start | bytes 589832 | tf_op jit(solution)/shard_map/ppermute | solution.py:284
  27.4 7.5 %collective-permute-start.9 = (f32[2,8,256]{2,1,0:T(8,128)S(1)}, f32[2,8,256]{2,1,0:T(8,128)S(1)}, u32[]{:S(2)}, u32[]{:S(2)}) collective-permute-start(f32[2,8,256]{2,1,0:T(8,128)S(1)} %get-tuple-element.24.own_ref), channel_id=1, source_target_pairs={{0,1},{1,0},{2,3},{3,2},{4,5},{5,4},{6,7},{7,6},{8,9},{9,8},{10,11... | collective-permute-start | bytes 49160 | tf_op jit(solution)/shard_map/ppermute | solution.py:284
  30.7 22.0 %all-to-all-start = ((bf16[32,8,768]{2,1,0:T(8,128)(2,1)}), bf16[32,8,768]{2,1,0:T(8,128)(2,1)S(1)}, u32[]{:S(2)}, u32[]{:S(2)}) async-start(bf16[32,8,768]{2,1,0:T(8,128)(2,1)} %bitcast.46), calls=%async_computation | async-start | bytes 786432 | tf_op jit(solution)/shard_map/all_to_all | solution.py:320
  35.0 12.8 %collective-permute-start.10 = (f32[2,8,256]{2,1,0:T(8,128)S(1)}, f32[2,8,256]{2,1,0:T(8,128)S(1)}, u32[]{:S(2)}, u32[]{:S(2)}) collective-permute-start(f32[2,8,256]{2,1,0:T(8,128)S(1)} %pad_maximum_fusion.8), channel_id=1, source_target_pairs={{0,4},{1,5},{2,6},{3,7},{4,0},{5,1},{6,2},{7,3},{8,12},{9,13},{10,... | collective-permute-start | bytes 49160 | tf_op jit(solution)/shard_map/ppermute | solution.py:284
  47.8 3.8 %collective-permute-start.11 = (f32[2,8,256]{2,1,0:T(8,128)S(1)}, f32[2,8,256]{2,1,0:T(8,128)S(1)}, u32[]{:S(2)}, u32[]{:S(2)}) collective-permute-start(f32[2,8,256]{2,1,0:T(8,128)S(1)} %pad_maximum_fusion.9), channel_id=1, source_target_pairs={{0,2},{1,3},{2,0},{3,1},{4,6},{5,7},{6,4},{7,5},{8,10},{9,11},{10,... | collective-permute-start | bytes 49160 | tf_op jit(solution)/shard_map/ppermute | solution.py:284

commit v5 on v4

--- a/solution.py
+++ b/solution.py
@@ -96,7 +96,8 @@
                 terms = g.astype(F32) * o_ref[:, at(to, h)].astype(F32)
                 delta = jnp.sum(terms, axis=1, keepdims=True)
                 for part, value in enumerate(split3(delta)):
-                    extra = jnp.where(lane == part * heads + h, value.astype(F32), extra)
+                    mine = lane == (3 * section + part) * heads + h
+                    extra = jnp.where(mine, value.astype(F32), extra)
                 out_ref[:, head_of(h)] = q_ref[:, at(to, h)]
                 out_ref[:, head_of(heads + 1 + h)] = g
             out_ref[:, head_of(heads)] = extra.astype(BF)
@@ -133,9 +134,15 @@
     return key_pos <= key_total - row_count + row
 
 
+def query_head(q_ref, h, here):
+    layers = (q_ref.shape[1] - LANES) // here
+    parts = [q_ref[:, pl.ds(i * here + h * HEAD_DIM, HEAD_DIM)] for i in range(layers)]
+    return jnp.concatenate(parts, axis=0)
+
+
 def stats_kernel(start, queries, keys, row_count, key_total):
-    m = queries.shape[0]
     key_count, here = keys.shape
+    m = queries.shape[0] * ((queries.shape[1] - LANES) // here)
     heads = here // HEAD_DIM
     slots = -(-heads // 8) * 8
     scaling = HEAD_DIM ** (-0.5)
@@ -145,7 +152,7 @@
         out_ref[...] = jnp.ones_like(out_ref)
         for h in range(heads):
             at = head_of(h)
-            s = jnp.where(visible, nt(k_ref[:, at], q_ref[:, at]) * scaling, masked_score)
+            s = jnp.where(visible, nt(k_ref[:, at], query_head(q_ref, h, here)) * scaling, masked_score)
             top = jnp.max(s, axis=0, keepdims=True)
             prob = jnp.where(visible, jnp.exp(s - top), 0.0)
             prob_ref[h] = prob
@@ -179,8 +186,14 @@
 
         slot = lax.broadcasted_iota(jnp.int32, (slots, LANES), 0)
         lane = lax.broadcasted_iota(jnp.int32, (slots, LANES), 1)
-        pick = (lane % heads == slot) & (lane < 3 * heads)
-        deltas = nt(jnp.where(pick, 1.0, 0.0).astype(BF), q_ref[:, pl.ds(here, LANES)])
+        width = 3 * heads
+        layers = m // q_ref.shape[0]
+        extra = q_ref[:, pl.ds(layers * here, LANES)]
+        spot = lax.broadcasted_iota(jnp.int32, extra.shape, 1)
+        parts = [jnp.where(spot // width == i, extra, jnp.zeros_like(extra)) for i in range(layers)]
+        pick = (lane % heads == slot) & (lane < layers * width)
+        pick = jnp.where(pick, 1.0, 0.0).astype(BF)
+        deltas = nt(pick, jnp.concatenate(parts, axis=0))
         sent = jnp.zeros((m, LANES), F32)
         for i in range(2):
             for part, value in enumerate(split3(own_ref[i])):
@@ -226,7 +239,7 @@
             row = share[h : h + 1, :]
             ds = (ds_ref[h].astype(F32) * row).astype(BF)
             prob = (p_ref[h] * row).astype(BF)
-            dk_ref[:, at] = nn(ds, q_ref[:, at]).astype(BF)
+            dk_ref[:, at] = nn(ds, query_head(q_ref, h, here)).astype(BF)
             dv_ref[:, at] = nn(prob, g_ref[:, at]).astype(BF)
 
     return pl.pallas_call(
@@ -325,8 +338,8 @@
     ctx_count = lax.axis_size("ctx")
     assert ctx_count & (ctx_count - 1) == 0
     assert sections & (sections - 1) == 0 and sections > 1
-    layers, rows, _ = queries.shape
-    assert layers == 1
+    layers, rows, features = queries.shape
+    assert layers == 1 and 3 * features // HEAD_DIM <= LANES
     key_count, here = cache_keys.shape
     row_count = rows * ctx_count
     key_total = key_count * ctx_count
@@ -346,10 +359,12 @@
     )
     start, keys, values = packed[sections:]
     swapped = swap_blocks(packed[:sections], "section")
-    query_all, grad_all = swapped[..., : here + LANES], swapped[..., here + LANES :]
-    query_all = spread_blocks(query_all, "ctx", down)
-    query_all = query_all.reshape(peers * rows, here + LANES)
-    grad_all = spread_blocks(grad_all, "ctx", down[:1] + down[1:][::-1])
+    deltas = sum(block[:, here : here + LANES] for block in swapped)
+    sent = jnp.concatenate([*(block[:, :here] for block in swapped), deltas], axis=1)
+    query_all = spread_blocks(sent[None], "ctx", down)
+    query_all = query_all.reshape(row_count, -1)
+    sent = jnp.stack([block[:, here + LANES :] for block in swapped])
+    grad_all = spread_blocks(sent, "ctx", down[:1] + down[1:][::-1])
     grad_all = grad_all.reshape(peers * rows, here)
 
     own, probs = stats_kernel(start, query_all, keys, row_count, key_total)

time: 53.9 us -> 53.6 us (level)
  no operation moved by 1% of the time
where the time goes in v5:
time: 53.6 us; the launch traced here: 53.3 us
  waiting for transfers between devices  25.2 us (47%)
  starting transfers between devices  21.6 us (40%)
  Pallas kernels  5.23 us (10%)
  between operations  0.83 us (2%)
    ppermute x12, waiting for transfers between devices, flip(): return lax.ppermute(value, axis, [(i, i ^ bit) for i in range(count)])  25.2 us
    ppermute x12, starting transfers between devices, flip(): return lax.ppermute(value, axis, [(i, i ^ bit) for i in range(count)])  17.3 us
    all_to_all x1, starting transfers between devices, exchange(): return lax.all_to_all(blocks, ('section', 'ctx'), 0, 0, tiled=True)  4.29 us
    pallas_call x1, Pallas kernels, query_kernel(): pl.pallas_call(body, in_specs=in_vmem(6), out_specs=[pl.BlockSpec(memory_...  1.67 us
    pallas_call x1, Pallas kernels, pack(): pl.pallas_call(body, in_specs=[pl.BlockSpec(memory_space=pl.ANY)] * 6, ou...  1.12 us
  transfers between devices with their start and end apart: 13, of which 10 were waited for; matrix products, arithmetic and copies ran while one was open for 1% of the time, Pallas kernels for 5%

profile of v5, /device:TPU:0, one launch (start us, length us, event | category | flops | bytes accessed | tf_op | source)
XLA Modules:
  0.0 53.3 jit_solution(8099545679221144898)
XLA Ops:
  0.6 1.1 %pack.1 = (bf16[8,1408]{1,0:T(8,128)(2,1)S(1)}, bf16[8,1408]{1,0:T(8,128)(2,1)S(1)}, bf16[8,1408]{1,0:T(8,128)(2,1)S(1)}, bf16[8,1408]{1,0:T(8,128)(2,1)S(1)}, s...) custom-call(s32[8]{0:T(128)} %order_hbm.1, bf16[128,640]{1,0:T(8,128)(2,1)} %k_hbm.1, ...), custom_call_target="tpu_custom_call" | custom-call | tf_op jit(solution)/shard_map/pack/pallas_call | solution.py:110
  1.8 2.5 %collective-permute-start = (bf16[8,1408]{1,0:T(8,128)(2,1)S(1)}, bf16[8,1408]{1,0:T(8,128)(2,1)S(1)}, u32[]{:S(2)}, u32[]{:S(2)}) collective-permute-start(bf16[8,1408]{1,0:T(8,128)(2,1)S(1)} %get-tuple-element.16), channel_id=1, source_target_pairs={{0,24},{8,16},{16,8},{24,0},{1,25},{9,17},{17,9},{25,1},{2,26},{10... | collective-permute-start | bytes 67592 | tf_op jit(solution)/shard_map/ppermute | solution.py:297
  4.2 0.6 %collective-permute-start.1 = (bf16[8,1408]{1,0:T(8,128)(2,1)S(1)}, bf16[8,1408]{1,0:T(8,128)(2,1)S(1)}, u32[]{:S(2)}, u32[]{:S(2)}) collective-permute-start(bf16[8,1408]{1,0:T(8,128)(2,1)S(1)} %get-tuple-element.17), channel_id=1, source_target_pairs={{0,16},{8,24},{16,0},{24,8},{1,17},{9,25},{17,1},{25,9},{2,18},{10... | collective-permute-start | bytes 67592 | tf_op jit(solution)/shard_map/ppermute | solution.py:297
  4.9 0.9 %collective-permute-done = bf16[8,1408]{1,0:T(8,128)(2,1)S(1)} collective-permute-done((bf16[8,1408]{1,0:T(8,128)(2,1)S(1)}, bf16[8,1408]{1,0:T(8,128)(2,1)S(1)}, u32[]{:S(2)}, u32[]{:S(2)}) %collective-permute-start) | collective-permute-done | bytes 22560 | tf_op jit(solution)/shard_map/ppermute | solution.py:297
  5.8 2.2 %collective-permute-done.1 = bf16[8,1408]{1,0:T(8,128)(2,1)S(1)} collective-permute-done((bf16[8,1408]{1,0:T(8,128)(2,1)S(1)}, bf16[8,1408]{1,0:T(8,128)(2,1)S(1)}, u32[]{:S(2)}, u32[]{:S(2)}) %collective-permute-start.1) | collective-permute-done | bytes 22560 | tf_op jit(solution)/shard_map/ppermute | solution.py:297
  8.1 2.7 %collective-permute-start.6 = (bf16[4,8,640]{2,1,0:T(8,128)(2,1)S(1)}, bf16[4,8,640]{2,1,0:T(8,128)(2,1)S(1)}, u32[]{:S(2)}, u32[]{:S(2)}) collective-permute-start(bf16[4,8,640]{2,1,0:T(8,128)(2,1)S(1)} %pad_maximum_fusion.6), channel_id=1, source_target_pairs={{0,4},{1,5},{2,6},{3,7},{4,0},{5,1},{6,2},{7,3},{8,12},{9,13},{10,... | collective-permute-start | bytes 122888 | tf_op jit(solution)/shard_map/ppermute | solution.py:297
  11.1 2.0 %collective-permute-done.6 = bf16[4,8,640]{2,1,0:T(8,128)(2,1)S(1)} collective-permute-done((bf16[4,8,640]{2,1,0:T(8,128)(2,1)S(1)}, bf16[4,8,640]{2,1,0:T(8,128)(2,1)S(1)}, u32[]{:S(2)}, u32[]{:S(2)}) %collective-permute-start.6) | collective-permute-done | bytes 40992 | tf_op jit(solution)/shard_map/ppermute | solution.py:297
  13.1 1.6 %collective-permute-start.7 = (bf16[4,2,8,640]{3,2,0,1:T(8,128)(2,1)S(1)}, bf16[4,2,8,640]{3,2,0,1:T(8,128)(2,1)S(1)}, u32[]{:S(2)}, u32[]{:S(2)}) collective-permute-start(bf16[4,2,8,640]{3,2,0,1:T(8,128)(2,1)S(1)} %pad_maximum_fusion.5), channel_id=1, source_target_pairs={{0,1},{1,0},{2,3},{3,2},{4,5},{5,4},{6,7},{7,6},{8,9},{9,8},{10,11... | collective-permute-start | bytes 245768 | tf_op jit(solution)/shard_map/ppermute | solution.py:297
  14.7 1.0 %collective-permute-done.3 = bf16[1,8,2688]{2,1,0:T(8,128)(2,1)S(1)} collective-permute-done((bf16[1,8,2688]{2,1,0:T(8,128)(2,1)S(1)}, bf16[1,8,2688]{2,1,0:T(8,128)(2,1)S(1)}, u32[]{:S(2)}, u32[]{:S(2)}) %collective-permute-start.3) | collective-permute-done | bytes 43040 | tf_op jit(solution)/shard_map/ppermute | solution.py:297
  15.8 1.6 %collective-permute-start.4 = (bf16[1,2,8,2688]{3,2,1,0:T(8,128)(2,1)S(1)}, bf16[1,2,8,2688]{3,2,1,0:T(8,128)(2,1)S(1)}, u32[]{:S(2)}, u32[]{:S(2)}) collective-permute-start(bf16[1,2,8,2688]{3,2,1,0:T(8,128)(2,1)S(1)} %pad_maximum_fusion.4), channel_id=1, source_target_pairs={{0,2},{1,3},{2,0},{3,1},{4,6},{5,7},{6,4},{7,5},{8,10},{9,11},{10,... | collective-permute-start | bytes 258056 | tf_op jit(solution)/shard_map/ppermute | solution.py:297
  17.7 2.0 %collective-permute-start.8 = (bf16[4,2,2,8,640]{4,3,0,1,2:T(8,128)(2,1)S(1)}, bf16[4,2,2,8,640]{4,3,0,1,2:T(8,128)(2,1)S(1)}, u32[]{:S(2)}, u32[]{:S(2)}) collective-permute-start(bf16[4,2,2,8,640]{4,3,0,1,2:T(8,128)(2,1)S(1)} %pad_maximum_fusion.3), channel_id=1, source_target_pairs={{0,2},{1,3},{2,0},{3,1},{4,6},{5,7},{6,4},{7,5},{8,10},{9,11},{10,... | collective-permute-start | bytes 491528 | tf_op jit(solution)/shard_map/ppermute | solution.py:297
  19.7 1.0 %collective-permute-done.4 = bf16[1,2,8,2688]{3,2,1,0:T(8,128)(2,1)S(1)} collective-permute-done((bf16[1,2,8,2688]{3,2,1,0:T(8,128)(2,1)S(1)}, bf16[1,2,8,2688]{3,2,1,0:T(8,128)(2,1)S(1)}, u32[]{:S(2)}, u32[]{:S(2)}) %collective-permute-start.4) | collective-permute-done | bytes 86048 | tf_op jit(solution)/shard_map/ppermute | solution.py:297
  20.7 1.6 %collective-permute-start.5 = (bf16[1,2,2,8,2688]{4,3,1,2,0:T(8,128)(2,1)S(1)}, bf16[1,2,2,8,2688]{4,3,1,2,0:T(8,128)(2,1)S(1)}, u32[]{:S(2)}, u32[]{:S(2)}) collective-permute-start(bf16[1,2,2,8,2688]{4,3,1,2,0:T(8,128)(2,1)S(1)} %pad_maximum_fusion.2), channel_id=1, source_target_pairs={{0,1},{1,0},{2,3},{3,2},{4,5},{5,4},{6,7},{7,6},{8,9},{9,8},{10,11... | collective-permute-start | bytes 516104 | tf_op jit(solution)/shard_map/ppermute | solution.py:297
  22.3 0.8 %collective-permute-done.8 = bf16[4,2,2,8,640]{4,3,0,1,2:T(8,128)(2,1)S(1)} collective-permute-done((bf16[4,2,2,8,640]{4,3,0,1,2:T(8,128)(2,1)S(1)}, bf16[4,2,2,8,640]{4,3,0,1,2:T(8,128)(2,1)S(1)}, u32[]{:S(2)}, u32[]{:S(2)}) %collective-permute-start.8) | collective-permute-done | bytes 163872 | tf_op jit(solution)/shard_map/ppermute | solution.py:297
  23.1 3.3 %collective-permute-done.5 = bf16[1,2,2,8,2688]{4,3,1,2,0:T(8,128)(2,1)S(1)} collective-permute-done((bf16[1,2,2,8,2688]{4,3,1,2,0:T(8,128)(2,1)S(1)}, bf16[1,2,2,8,2688]{4,3,1,2,0:T(8,128)(2,1)S(1)}, u32[]{:S(2)}, u32[]{:S(2)}) %collective-permute-start.5) | collective-permute-done | bytes 172064 | tf_op jit(solution)/shard_map/ppermute | solution.py:297
  26.5 0.4 stats.1
  27.0 1.6 %collective-permute-start.9 = (f32[2,8,256]{2,1,0:T(8,128)S(1)}, f32[2,8,256]{2,1,0:T(8,128)S(1)}, u32[]{:S(2)}, u32[]{:S(2)}) collective-permute-start(f32[2,8,256]{2,1,0:T(8,128)S(1)} %get-tuple-element.24.own_ref), channel_id=1, source_target_pairs={{0,1},{1,0},{2,3},{3,2},{4,5},{5,4},{6,7},{7,6},{8,9},{9,8},{10,11... | collective-permute-start | bytes 49160 | tf_op jit(solution)/shard_map/ppermute | solution.py:297
  28.6 1.7 %query_gradients.1 = (bf16[256,768]{1,0:T(8,128)(2,1)}, bf16[5,128,256]{2,1,0:T(8,128)(2,1)S(1)}) custom-call(bf16[64,2688]{1,0:T(8,128)(2,1)S(1)} %bitcast.44, bf16[256,640]{1,0:T(8,128)(2,1)S(1)} %bitcast.46, bf16[128,640]{1,0:T(8,128)(2,1)S(1)} %get-tuple-element.20.k_ref, bf16[128,640]{1,0:T(8,128)(2,1)S(1)} %get-tuple-element.21.v_ref, ...), custom_call_target="tpu_custom_call" | custom-call | tf_op jit(solution)/shard_map/query_gradients/pallas_call | solution.py:215
  30.3 4.3 %all-to-all-start = ((bf16[32,8,768]{2,1,0:T(8,128)(2,1)}), bf16[32,8,768]{2,1,0:T(8,128)(2,1)S(1)}, u32[]{:S(2)}, u32[]{:S(2)}) async-start(bf16[32,8,768]{2,1,0:T(8,128)(2,1)} %bitcast.49), calls=%async_computation | async-start | bytes 786432 | tf_op jit(solution)/shard_map/all_to_all | solution.py:333
  34.6 2.7 %collective-permute-start.10 = (f32[2,8,256]{2,1,0:T(8,128)S(1)}, f32[2,8,256]{2,1,0:T(8,128)S(1)}, u32[]{:S(2)}, u32[]{:S(2)}) collective-permute-start(f32[2,8,256]{2,1,0:T(8,128)S(1)} %pad_maximum_fusion.7), channel_id=1, source_target_pairs={{0,4},{1,5},{2,6},{3,7},{4,0},{5,1},{6,2},{7,3},{8,12},{9,13},{10,... | collective-permute-start | bytes 49160 | tf_op jit(solution)/shard_map/ppermute | solution.py:297
  37.4 10.1 %collective-permute-done.10 = f32[2,8,256]{2,1,0:T(8,128)S(1)} collective-permute-done((f32[2,8,256]{2,1,0:T(8,128)S(1)}, f32[2,8,256]{2,1,0:T(8,128)S(1)}, u32[]{:S(2)}, u32[]{:S(2)}) %collective-permute-start.10) | collective-permute-done | bytes 16416 | tf_op jit(solution)/shard_map/ppermute | solution.py:297
  47.5 3.7 %collective-permute-done.11 = f32[2,8,256]{2,1,0:T(8,128)S(1)} collective-permute-done((f32[2,8,256]{2,1,0:T(8,128)S(1)}, f32[2,8,256]{2,1,0:T(8,128)S(1)}, u32[]{:S(2)}, u32[]{:S(2)}) %collective-permute-start.11) | collective-permute-done | bytes 16416 | tf_op jit(solution)/shard_map/ppermute | solution.py:297
  51.3 1.0 %cache_gradients.1 = (bf16[128,640]{1,0:T(8,128)(2,1)}, bf16[128,640]{1,0:T(8,128)(2,1)}) custom-call(bf16[64,2688]{1,0:T(8,128)(2,1)S(1)} %bitcast.45, bf16[256,640]{1,0:T(8,128)(2,1)S(1)} %bitcast.47, f32[5,128,256]{2,1,0:T(8,128)S(1)} %get-tuple-element.23.p_ref, bf16[5,128,256]{2,1,0:T(8,128)(2,1)S(1)} %get-tuple-element.26.ds_ref, ...), custom_call_target="tpu_custom_call" | custom-call | tf_op jit(solution)/shard_map/cache_gradients/pallas_call | solution.py:245
  52.3 1.0 %combine.1 = bf16[8,2560]{1,0:T(8,128)(2,1)} custom-call(bf16[256,768]{1,0:T(8,128)(2,1)S(1)} %bitcast.48), custom_call_target="tpu_custom_call" | custom-call | tf_op jit(solution)/shard_map/combine/pallas_call | solution.py:277
  (34 shorter events, 1.2 us)
Async XLA Ops:
  1.8 4.0 %collective-permute-start = (bf16[8,1408]{1,0:T(8,128)(2,1)S(1)}, bf16[8,1408]{1,0:T(8,128)(2,1)S(1)}, u32[]{:S(2)}, u32[]{:S(2)}) collective-permute-start(bf16[8,1408]{1,0:T(8,128)(2,1)S(1)} %get-tuple-element.16), channel_id=1, source_target_pairs={{0,24},{8,16},{16,8},{24,0},{1,25},{9,17},{17,9},{25,1},{2,26},{10... | collective-permute-start | bytes 67592 | tf_op jit(solution)/shard_map/ppermute | solution.py:297
  4.2 3.8 %collective-permute-start.1 = (bf16[8,1408]{1,0:T(8,128)(2,1)S(1)}, bf16[8,1408]{1,0:T(8,128)(2,1)S(1)}, u32[]{:S(2)}, u32[]{:S(2)}) collective-permute-start(bf16[8,1408]{1,0:T(8,128)(2,1)S(1)} %get-tuple-element.17), channel_id=1, source_target_pairs={{0,16},{8,24},{16,0},{24,8},{1,17},{9,25},{17,1},{25,9},{2,18},{10... | collective-permute-start | bytes 67592 | tf_op jit(solution)/shard_map/ppermute | solution.py:297
  4.9 3.2 %collective-permute-start.2 = (bf16[8,1408]{1,0:T(8,128)(2,1)S(1)}, bf16[8,1408]{1,0:T(8,128)(2,1)S(1)}, u32[]{:S(2)}, u32[]{:S(2)}) collective-permute-start(bf16[8,1408]{1,0:T(8,128)(2,1)S(1)} %get-tuple-element.18), channel_id=1, source_target_pairs={{0,8},{8,0},{16,24},{24,16},{1,9},{9,1},{17,25},{25,17},{2,10},{10... | collective-permute-start | bytes 67592 | tf_op jit(solution)/shard_map/ppermute | solution.py:297
  8.1 5.0 %collective-permute-start.6 = (bf16[4,8,640]{2,1,0:T(8,128)(2,1)S(1)}, bf16[4,8,640]{2,1,0:T(8,128)(2,1)S(1)}, u32[]{:S(2)}, u32[]{:S(2)}) collective-permute-start(bf16[4,8,640]{2,1,0:T(8,128)(2,1)S(1)} %pad_maximum_fusion.6), channel_id=1, source_target_pairs={{0,4},{1,5},{2,6},{3,7},{4,0},{5,1},{6,2},{7,3},{8,12},{9,13},{10,... | collective-permute-start | bytes 122888 | tf_op jit(solution)/shard_map/ppermute | solution.py:297
  10.8 4.9 %collective-permute-start.3 = (bf16[1,8,2688]{2,1,0:T(8,128)(2,1)S(1)}, bf16[1,8,2688]{2,1,0:T(8,128)(2,1)S(1)}, u32[]{:S(2)}, u32[]{:S(2)}) collective-permute-start(bf16[1,8,2688]{2,1,0:T(8,128)(2,1)S(1)} %bitcast.50), channel_id=1, source_target_pairs={{0,4},{1,5},{2,6},{3,7},{4,0},{5,1},{6,2},{7,3},{8,12},{9,13},{10,... | collective-permute-start | bytes 129032 | tf_op jit(solution)/shard_map/ppermute | solution.py:297
  13.1 4.5 %collective-permute-start.7 = (bf16[4,2,8,640]{3,2,0,1:T(8,128)(2,1)S(1)}, bf16[4,2,8,640]{3,2,0,1:T(8,128)(2,1)S(1)}, u32[]{:S(2)}, u32[]{:S(2)}) collective-permute-start(bf16[4,2,8,640]{3,2,0,1:T(8,128)(2,1)S(1)} %pad_maximum_fusion.5), channel_id=1, source_target_pairs={{0,1},{1,0},{2,3},{3,2},{4,5},{5,4},{6,7},{7,6},{8,9},{9,8},{10,11... | collective-permute-start | bytes 245768 | tf_op jit(solution)/shard_map/ppermute | solution.py:297
  15.8 4.9 %collective-permute-start.4 = (bf16[1,2,8,2688]{3,2,1,0:T(8,128)(2,1)S(1)}, bf16[1,2,8,2688]{3,2,1,0:T(8,128)(2,1)S(1)}, u32[]{:S(2)}, u32[]{:S(2)}) collective-permute-start(bf16[1,2,8,2688]{3,2,1,0:T(8,128)(2,1)S(1)} %pad_maximum_fusion.4), channel_id=1, source_target_pairs={{0,2},{1,3},{2,0},{3,1},{4,6},{5,7},{6,4},{7,5},{8,10},{9,11},{10,... | collective-permute-start | bytes 258056 | tf_op jit(solution)/shard_map/ppermute | solution.py:297
  17.7 5.4 %collective-permute-start.8 = (bf16[4,2,2,8,640]{4,3,0,1,2:T(8,128)(2,1)S(1)}, bf16[4,2,2,8,640]{4,3,0,1,2:T(8,128)(2,1)S(1)}, u32[]{:S(2)}, u32[]{:S(2)}) collective-permute-start(bf16[4,2,2,8,640]{4,3,0,1,2:T(8,128)(2,1)S(1)} %pad_maximum_fusion.3), channel_id=1, source_target_pairs={{0,2},{1,3},{2,0},{3,1},{4,6},{5,7},{6,4},{7,5},{8,10},{9,11},{10,... | collective-permute-start | bytes 491528 | tf_op jit(solution)/shard_map/ppermute | solution.py:297
  20.7 5.6 %collective-permute-start.5 = (bf16[1,2,2,8,2688]{4,3,1,2,0:T(8,128)(2,1)S(1)}, bf16[1,2,2,8,2688]{4,3,1,2,0:T(8,128)(2,1)S(1)}, u32[]{:S(2)}, u32[]{:S(2)}) collective-permute-start(bf16[1,2,2,8,2688]{4,3,1,2,0:T(8,128)(2,1)S(1)} %pad_maximum_fusion.2), channel_id=1, source_target_pairs={{0,1},{1,0},{2,3},{3,2},{4,5},{5,4},{6,7},{7,6},{8,9},{9,8},{10,11... | collective-permute-start | bytes 516104 | tf_op jit(solution)/shard_map/ppermute | solution.py:297
  27.0 7.6 %collective-permute-start.9 = (f32[2,8,256]{2,1,0:T(8,128)S(1)}, f32[2,8,256]{2,1,0:T(8,128)S(1)}, u32[]{:S(2)}, u32[]{:S(2)}) collective-permute-start(f32[2,8,256]{2,1,0:T(8,128)S(1)} %get-tuple-element.24.own_ref), channel_id=1, source_target_pairs={{0,1},{1,0},{2,3},{3,2},{4,5},{5,4},{6,7},{7,6},{8,9},{9,8},{10,11... | collective-permute-start | bytes 49160 | tf_op jit(solution)/shard_map/ppermute | solution.py:297
  30.3 22.1 %all-to-all-start = ((bf16[32,8,768]{2,1,0:T(8,128)(2,1)}), bf16[32,8,768]{2,1,0:T(8,128)(2,1)S(1)}, u32[]{:S(2)}, u32[]{:S(2)}) async-start(bf16[32,8,768]{2,1,0:T(8,128)(2,1)} %bitcast.49), calls=%async_computation | async-start | bytes 786432 | tf_op jit(solution)/shard_map/all_to_all | solution.py:333
  34.6 12.8 %collective-permute-start.10 = (f32[2,8,256]{2,1,0:T(8,128)S(1)}, f32[2,8,256]{2,1,0:T(8,128)S(1)}, u32[]{:S(2)}, u32[]{:S(2)}) collective-permute-start(f32[2,8,256]{2,1,0:T(8,128)S(1)} %pad_maximum_fusion.7), channel_id=1, source_target_pairs={{0,4},{1,5},{2,6},{3,7},{4,0},{5,1},{6,2},{7,3},{8,12},{9,13},{10,... | collective-permute-start | bytes 49160 | tf_op jit(solution)/shard_map/ppermute | solution.py:297
  47.5 3.8 %collective-permute-start.11 = (f32[2,8,256]{2,1,0:T(8,128)S(1)}, f32[2,8,256]{2,1,0:T(8,128)S(1)}, u32[]{:S(2)}, u32[]{:S(2)}) collective-permute-start(f32[2,8,256]{2,1,0:T(8,128)S(1)} %pad_maximum_fusion.8), channel_id=1, source_target_pairs={{0,2},{1,3},{2,0},{3,1},{4,6},{5,7},{6,4},{7,5},{8,10},{9,11},{10,... | collective-permute-start | bytes 49160 | tf_op jit(solution)/shard_map/ppermute | solution.py:297
